TPU v7x, 256 devices: a whole 4x4x8 slice. The times are simulated.
256 devices in a mesh: tok: 4 (over y), smp: 64 (over x, z, core).
Axes of the slice: x: 4, y: 4, z: 8, core: 2. Of those that a mesh axis runs over, the one named last changes fastest.
Arguments:
- row_table: float32 [8, 16384, 384], P('tok', 'smp'), may hold values from -6 to 6
- row_accum: float32 [8, 16384], P('tok', 'smp'), may hold values from 0.0001 to 0.01
- last_step: int32 [8, 16384], P('tok', 'smp'), may hold values from 0 to 47
- step_now: int32 [1], replicated, may hold values from 48 to 63
- row_ids: int32 [8, 64, 64, 2], P('tok', 'smp'), may hold values from 0 to 255, as said below
- row_counts: int32 [8, 64, 64], P('tok', 'smp'), may hold values from 1 to 2, as said below
- sample_slots: int32 [8, 16384], P(None, 'smp'), may hold values from 0 to 127, as said below
- labels: int32 [16384], P('smp'), may hold values 0 or 1
- up_weight: bfloat16 [384, 8, 1536], P('smp', 'tok'), may hold values from -0.3125 to 0.3125
- down_weight: bfloat16 [384, 8, 1536], P('smp', 'tok'), may hold values from -0.15625 to 0.15625
- out_weight: float32 [8, 384], P('tok'), may hold values from -0.3125 to 0.3125
Outputs:
- new_table: float32 [8, 16384, 384], P('tok', 'smp')
- new_accum: float32 [8, 16384], P('tok', 'smp')
- grad_down: float32 [384, 8, 1536], P('smp', 'tok')
- logits: float32 [16384], P('smp')
Inputs may be any that keep to these rules, and one draw needn't show every extreme that they name: The first row_counts[t, o, g] entries of each list are distinct; later entries are padding; every token and owner has a list of 2 valid entries for some group. `row_ids`: row numbers within the owner's shard. `sample_slots`: each slot o * 2 + c names a valid entry c < row_counts[t, o, s // 256]. `last_step`: each row's last step is before step_now.
All inputs are finite; a program needn't handle non-finite values. No bound on the sum of `labels` on one device may be relied on, other than what follows from the above.
Results may differ from a plain program's by a relative error of at most 0.0021.
Values may be sent and summed in bfloat16 or wider, within the bound.
No kernel may reach another device: no remote copies, remote signals or barrier semaphores. Data moves between devices by JAX's collectives and lax.ppermute only.
A program may use at most 64 MiB of HBM per device.

v0:
```python
import math

import jax
import jax.numpy as jnp
import numpy as np
from jax import lax
from jax.experimental import pallas as pl
from jax.experimental.pallas import tpu as pltpu
from jax.sharding import Mesh
from jax.sharding import PartitionSpec as P


decay_log = math.log(0.98)
learn_rate = 0.2
norm_eps = 1e-05
f32 = jnp.float32
bf16 = jnp.bfloat16
f16 = jnp.float16
i32 = jnp.int32


NN = (((1,), (0,)), ((), ()))
NT = (((1,), (1,)), ((), ()))
VM = pl.BlockSpec(memory_space=pltpu.VMEM)
SM = pl.BlockSpec(memory_space=pltpu.SMEM)
ANY = pl.BlockSpec(memory_space=pl.ANY)
HBM = pl.BlockSpec(memory_space=pltpu.HBM)


def dot(a, b, dims=NN):
    return lax.dot_general(a, b, dims, preferred_element_type=f32)


def split(v):
    hi = v.astype(bf16)
    return hi, (v - hi.astype(f32)).astype(bf16)


def dot2(v, b, dims=NN):
    hi, lo = split(v)
    return dot(hi, b, dims) + dot(lo, b, dims)


def iota(shape, dim):
    return lax.broadcasted_iota(i32, shape, dim)


def call(body, outs, name, scratch=(), n_in=0, smem=0, flops=0, nbytes=0, room=8, away=0):
    return pl.pallas_call(
        body,
        out_shape=outs,
        in_specs=[SM] * smem + [HBM if name == "lookup" else ANY] * away + [VM] * (n_in - smem - away),
        out_specs=jax.tree.map(lambda _: VM, outs),
        scratch_shapes=list(scratch),
        compiler_params=pltpu.CompilerParams(vmem_limit_bytes=room * 2**20),
        cost_estimate=pl.CostEstimate(flops=flops, bytes_accessed=nbytes, transcendentals=0),
    )


def sds(shape, dtype=f32):
    return jax.ShapeDtypeStruct(shape, dtype)


def slot_columns(tab, cols):
    groups = tab.shape[1]
    col = iota((1, cols), 1)
    chip, tok, grp, slot = col // 8, (col // 4) % 2, (col // 2) % 2, col % 2
    pick = (iota((groups, cols), 0) == chip * 2 + grp).astype(f32)
    every = lax.dot_general(tab, pick, NN, preferred_element_type=f32, precision=lax.Precision.HIGHEST)
    keep = iota((4, cols), 0) == tok * 2 + slot
    return jnp.sum(jnp.where(keep, every, 0.0), axis=0, keepdims=True), tok, slot


def lookup_body(step_ref, table_hbm, last_hbm, ids_hbm, out_ref, table_ref, last_ref, ids_ref, sems):
    copies = [
        pltpu.make_async_copy(source, target, sems.at[k])
        for k, (source, target) in enumerate(((ids_hbm, ids_ref), (last_hbm, last_ref), (table_hbm, table_ref)))
    ]
    for copy in copies:
        copy.start()
    toks, rows, width = table_ref.shape
    cols = out_ref.shape[0]
    copies[0].wait()
    ids, tok, _ = slot_columns(ids_ref[...].astype(f32), cols)
    ids = ids + tok.astype(f32) * rows
    column = jnp.transpose(jnp.broadcast_to(ids, (8, cols)))[:, 0:1]
    copies[1].wait()
    weights = []
    for j in range(toks):
        elapsed = (step_ref[0] - last_ref[j : j + 1, :]).astype(f32)
        factor = jnp.exp(elapsed * decay_log)
        hit = iota((cols, rows), 1).astype(f32) + (j * rows) == column
        weights.append(jnp.where(hit, factor, 0.0))
    copies[2].wait()
    total = jnp.zeros((cols, width), f32)
    for j in range(toks):
        total = total + lax.dot_general(
            weights[j], table_ref[j], NN, preferred_element_type=f32, precision=lax.Precision.HIGHEST
        )
    out_ref[...] = total


def list_targets(slots, half):
    group = (iota(slots.shape, 1) >= half).astype(i32)
    return (slots // 2) * 4 + group * 2 + slots % 2


def place_body(target_ref, place_ref):
    _, lines, width = place_ref.shape
    for k in range(2):
        place_ref[k] = (iota((lines, width), 1) == target_ref[:, k : k + 1]).astype(bf16)


def own_target(targets, token):
    return jnp.sum(jnp.where(iota(targets.shape, 0) == token, targets, 0), axis=0, keepdims=True)


def forward_body(
    where_ref, own_ref, heads_ref, slots_ref, head_ref, order_ref, z_ref, xp_ref, xm_ref, xa_ref, xb_ref,
    normed_in_ref, inv_in_ref, active_ref, slope_ref, normed_out_ref, inv_out_ref, logit_ref, up_ref, down_ref,
    target_ref, all_ref, total_ref, input_ref, choice_ref,
):
    start = 0
    for ref in (z_ref, xp_ref, xm_ref, xa_ref, xb_ref):
        all_ref[start : start + ref.shape[0]] = ref[...]
        start += ref.shape[0]
    width, lists = own_ref.shape
    samples = slots_ref.shape[1]
    toks = slots_ref.shape[0] // 2
    head = width // toks
    rows, hidden = all_ref.shape
    for k in range(2):
        choice_ref[k * width : (k + 1) * width] = (iota((width, rows), 0) == order_ref[k : k + 1, :]).astype(bf16)
    targets = list_targets(slots_ref[0:toks, :], samples // 2)
    target_ref[...] = targets
    row = iota((lists, samples), 0)
    mixed = []
    for t in range(toks):
        one = (row == targets[t : t + 1, :]).astype(bf16)
        mixed.append(dot2(heads_ref[t * head : (t + 1) * head, :], one))
    one_own = (row == own_target(targets, where_ref[0])).astype(bf16)
    value = dot2(own_ref[...], one_own) + jnp.concatenate(mixed, axis=0)
    centre = jnp.mean(value, axis=0, keepdims=True)
    shifted = value - centre
    inverse = lax.rsqrt(jnp.mean(shifted * shifted, axis=0, keepdims=True) + norm_eps)
    normed = shifted * inverse
    normed_in_ref[...] = normed
    inv_in_ref[...] = inverse
    input_ref[...] = jnp.transpose(normed.astype(bf16))
    total_ref[...] = normed
    chunk = 256

    @pl.loop(0, hidden // chunk)
    def _(i):
        cols = pl.ds(pl.multiple_of(i * chunk, chunk), chunk)
        both = dot(choice_ref[...], all_ref[:, cols]).astype(bf16)
        up, down = both[:width], both[width:]
        up_ref[:, cols] = up
        down_ref[:, cols] = down
        pre = dot(input_ref[...], up)
        cumulative = 0.5 * (1.0 + lax.erf(pre * (1.0 / math.sqrt(2.0))))
        density = jnp.exp(-0.5 * pre * pre) * (1.0 / math.sqrt(2.0 * math.pi))
        active = (pre * cumulative).astype(bf16)
        active_ref[:, cols] = active
        slope_ref[:, cols] = cumulative + pre * density
        total_ref[...] += dot(down, active, NT)

    value = total_ref[...]
    centre = jnp.mean(value, axis=0, keepdims=True)
    shifted = value - centre
    inverse = lax.rsqrt(jnp.mean(shifted * shifted, axis=0, keepdims=True) + norm_eps)
    normed = shifted * inverse
    normed_out_ref[...] = normed
    inv_out_ref[...] = inverse
    logit_ref[...] = jnp.sum(normed * head_ref[...], axis=0, keepdims=True)


def norm_back(grad_in, normed, inverse):
    first = jnp.mean(grad_in, axis=0, keepdims=True)
    second = jnp.mean(grad_in * normed, axis=0, keepdims=True)
    return inverse * (grad_in - first - normed * second)


def grad_down_body(
    place_ref, logit_ref, label_ref, head_ref, normed_out_ref, inv_out_ref, active_ref,
    grad_sum_ref, grad_out_ref, kept_ref, next_ref, far_ref, last_ref, padded_ref,
):
    dlogit = jax.nn.sigmoid(logit_ref[...]) - label_ref[...]
    grad = norm_back(dlogit * head_ref[...], normed_out_ref[...], inv_out_ref[...])
    grad_sum_ref[...] = grad
    rounded = grad.astype(bf16)
    grad_out_ref[...] = jnp.transpose(rounded)
    lines, half = kept_ref.shape
    for k in range(2):
        padded_ref[k] = dot(place_ref[k], rounded).astype(bf16)
    chunk = 256

    @pl.loop(0, half // chunk)
    def _(i):
        cols = pl.ds(pl.multiple_of(i * chunk, chunk), chunk)
        more = pl.ds(pl.multiple_of(half + i * chunk, chunk), chunk)
        value = dot(padded_ref[0], active_ref[:, cols]) + dot(padded_ref[1], active_ref[:, more])
        kept_ref[:, cols] = value[0:lines]
        next_ref[:, cols] = value[lines : 2 * lines].astype(bf16)
        far_ref[:, cols] = value[2 * lines : 3 * lines].astype(bf16)
        last_ref[:, cols] = value[3 * lines :].astype(bf16)


def grad_rows_body(
    where_ref, target_ref, grad_sum_ref, grad_out_ref, slope_ref, up_ref, down_ref, normed_in_ref, inv_in_ref,
    own_ref, back_ref, total_ref,
):
    lists, width = own_ref.shape
    toks, samples = target_ref.shape
    head = width // toks
    total_ref[...] = grad_sum_ref[...]
    chunk = 256

    @pl.loop(0, slope_ref.shape[1] // chunk)
    def _(i):
        cols = pl.ds(pl.multiple_of(i * chunk, chunk), chunk)
        grad = dot(grad_out_ref[...], down_ref[:, cols])
        grad_pre = (grad * slope_ref[:, cols]).astype(bf16)
        total_ref[...] += dot(up_ref[:, cols], grad_pre, NT)

    mixed = norm_back(total_ref[...], normed_in_ref[...], inv_in_ref[...])
    targets = target_ref[...]
    row = iota((lists, samples), 0)
    one_own = (row == own_target(targets, where_ref[0])).astype(bf16)
    hi, lo = split(mixed)
    own_ref[...] = dot(one_own, hi, NT) + dot(one_own, lo, NT)
    for t in range(toks):
        one = (row == targets[t : t + 1, :]).astype(bf16)
        span = slice(t * head, (t + 1) * head)
        back_ref[span, :] = (dot(hi[span], one, NT) + dot(lo[span], one, NT)).astype(bf16)


def list_body(own_ref, returned_ref, out_ref):
    returned = jnp.transpose(returned_ref[...].astype(f32))
    out_ref[...] = (own_ref[...] + returned).astype(bf16).reshape(out_ref.shape)


def update_body(
    step_ref, table_ref, accum_ref, last_ref, ids_ref, counts_ref, back_ref,
    table_out_ref, accum_out_ref,
):
    toks, rows, width = table_ref.shape
    cols = back_ref.shape[0] * back_ref.shape[1]
    ids, tok, slot = slot_columns(ids_ref[...].astype(f32), cols)
    counts = counts_ref[...].astype(f32)
    four = jnp.concatenate([counts[0:1], counts[0:1], counts[1:2], counts[1:2]], axis=0)
    have, _, _ = slot_columns(four, cols)
    valid = slot.astype(f32) < have
    row = iota((rows, cols), 0).astype(f32)
    back = back_ref[...].astype(f32).reshape(cols, width).astype(bf16)
    for j in range(toks):
        named = jnp.where((tok == j) & valid, ids, -1.0)
        hit = (row == named).astype(f32)
        grads = dot(hit.astype(bf16), back)
        square = grads * grads
        touched = jnp.max(hit, axis=1, keepdims=True) > 0.0
        flat = jnp.concatenate(
            [last_ref[j : j + 1, :].astype(f32), accum_ref[j : j + 1, :], jnp.zeros((6, rows), f32)], axis=0
        )
        upright = jnp.transpose(flat)
        factor = jnp.exp((step_ref[0].astype(f32) - upright[:, 0:1]) * decay_log)
        accum = upright[:, 1:2] + jnp.mean(square, axis=1, keepdims=True)
        wide = jnp.transpose(jnp.broadcast_to(accum, (rows, 8)))
        accum_out_ref[j : j + 1, :] = wide[0:1, :]
        table = table_ref[j]
        updated = table * factor - learn_rate * grads * lax.rsqrt(accum)
        table_out_ref[j] = jnp.where(touched, updated, table)


def ring(value, axis, size, shift):
    return lax.ppermute(value, axis, [(i, (i + shift) % size) for i in range(size)])


def flip(value, axis, size, bit):
    return lax.ppermute(value, axis, [(i, i ^ bit) for i in range(size)])


def weight_order(x, z, core, n_x, n_z, steps_z, part):
    block = part // n_z
    third = block // 4
    line = np.arange(4 * part)
    step_x = np.array([0, -1, 1, 2])[line // part]
    step_z = np.asarray(steps_z)[(line % part) // block]
    inner = line % block
    other = inner // (2 * third)
    is_down = (inner // third) % 2
    r = inner % third
    chip = ((x + step_x + n_x) % n_x) * n_z + (z + step_z + n_z) % n_z
    owner = jnp.where(core == 0, other, 1 - other)
    target = (chip * 2 + owner) * third + r
    return jnp.stack([jnp.where(is_down == 0, target, -1), jnp.where(is_down == 1, target, -1)]).astype(i32)


def place_order(x, z, n_x, n_z, third):
    block = 4 * third
    line = np.arange(n_x * n_z * block)
    step_x, pos, inner = line // (n_z * block), line // block % n_z, line % block
    chip = (x + step_x) % n_x * n_z + (z ^ (pos // 2 + pos % 2 * (n_z // 2)))
    row = chip * 2 * third + inner % (2 * third)
    second = inner // (2 * third)
    return jnp.stack([jnp.where(second == 0, row, -1), jnp.where(second == 1, row, -1)], axis=1).astype(i32)


def on_device(
    row_table, row_accum, last_step, step_now, row_ids, row_counts, sample_slots, labels, up_weight, down_weight, out_weight
):
    n_tok, n_x, n_z = lax.axis_size("tok"), lax.axis_size("x"), lax.axis_size("z")
    _, _, width = row_table.shape
    toks, batch = sample_slots.shape
    groups, capacity = row_ids.shape[2:]
    head = width // toks
    hidden = up_weight.shape[2]
    lists = 2 * groups * capacity
    samples = 2 * batch
    core = lax.axis_index("core")
    token = lax.axis_index("tok") * 2 + core

    ids = row_ids[:, 0].transpose(0, 2, 1).reshape(2 * capacity, groups)
    looked = call(
        lookup_body,
        sds((lists, width)),
        "lookup",
        scratch=(
            pltpu.VMEM(row_table.shape, f32), pltpu.VMEM(last_step.shape, i32), pltpu.VMEM(ids.shape, i32),
            pltpu.SemaphoreType.DMA((3,)),
        ),
        n_in=4, smem=1, flops=10**9, nbytes=2 * 10**6, away=3, room=48,
    )(step_now, row_table, last_step, ids)
    sent = looked.astype(f16).reshape(groups, 2 * capacity, width)
    got = lax.all_to_all(sent, ("x", "z", "core"), 0, 0, tiled=True)
    own = got.reshape(lists, width).T
    heads = lax.all_to_all(own.reshape(toks, head, lists), ("tok", "core"), 0, 0, tiled=True)
    heads = heads.reshape(width, lists).astype(f32)
    own = own.astype(f32)

    both = jnp.concatenate([up_weight, down_weight], axis=0)
    keep = jnp.where(core == 0, both[:, 0], both[:, 1])
    give = jnp.where(core == 0, both[:, 1], both[:, 0])
    piece = jnp.concatenate([keep, flip(give, "core", 2, 1)], axis=0)

    mine = jnp.concatenate([sample_slots, labels[None], jnp.zeros((toks - 1, batch), i32)], axis=0)
    theirs = flip(mine, "core", 2, 1)
    slots = jnp.where(core == 0, jnp.concatenate([mine, theirs], axis=1), jnp.concatenate([theirs, mine], axis=1))
    label_row = slots[toks : toks + 1].astype(f32)
    before, after = ring(piece, "z", n_z, 1), ring(piece, "z", n_z, -1)
    pair = jnp.concatenate([before, piece], axis=0)
    three = jnp.concatenate([before, piece, after], axis=0)
    far_before, far_after = ring(three, "z", n_z, 3), ring(pair, "z", n_z, -3)
    line = jnp.concatenate([three, far_before, far_after], axis=0)
    steps_z = (-1, 0, 1, -4, -3, -2, 2, 3)
    part = line.shape[0]
    x_before, x_after = ring(line, "x", n_x, 1), ring(line, "x", n_x, -1)
    far_a = ring(x_before[: part // 2], "x", n_x, 1)
    far_b = ring(x_after[part // 2 :], "x", n_x, -1)
    order = weight_order(lax.axis_index("x"), lax.axis_index("z"), core, n_x, n_z, steps_z, part)
    third = width // (n_x * n_z * 2)
    lines = n_z * 4 * third
    target = place_order(lax.axis_index("x"), lax.axis_index("z"), n_x, n_z, third)
    place = call(place_body, sds((2, n_x * lines, width), bf16), "place", n_in=1, flops=10**6, nbytes=10**6)(target)

    where = token.reshape(1).astype(i32)
    head_weight = jnp.where(core == 0, out_weight[0], out_weight[1])[:, None]
    full = (samples, hidden)
    weight = sds((width, hidden), bf16)
    normed_in, inv_in, active, slope, normed_out, inv_out, partial, up, down, targets = call(
        forward_body,
        (
            sds((width, samples)), sds((1, samples)), sds(full, bf16), sds(full),
            sds((width, samples)), sds((1, samples)), sds((1, samples)), weight, weight, sds((toks, samples), i32),
        ),
        "forward",
        scratch=(
            pltpu.VMEM((4 * part, hidden), bf16), pltpu.VMEM((width, samples), f32), pltpu.VMEM((samples, width), bf16),
            pltpu.VMEM((2 * width, 4 * part), bf16),
        ),
        n_in=11, smem=1, flops=4 * 10**9, nbytes=10**7, room=24,
    )(where, own, heads, slots, head_weight, order, line, x_before, x_after, far_a, far_b)
    logits = partial + flip(partial, "core", 2, 1)
    there = [flip(logits, "tok", n_tok, k) for k in (1, 2, 3)]
    logits = (logits + there[0]) + (there[1] + there[2])

    block = (lines, hidden // 2)
    grad_sum, grad_out, kept, *away = call(
        grad_down_body,
        (sds((width, samples)), sds((samples, width), bf16), sds(block), sds(block, bf16), sds(block, bf16), sds(block, bf16)),
        "grad_down",
        scratch=(pltpu.VMEM((2, n_x * lines, samples), bf16),),
        n_in=7, flops=2 * 10**9, nbytes=5 * 10**6,
    )(place, logits, label_row, head_weight, normed_out, inv_out, active)
    come = [ring(v, "x", n_x, k + 1) for k, v in enumerate(away)]
    pair = 8 * third
    total = kept + sum(v.astype(f32) for v in come)
    total = [total[k * pair : (k + 1) * pair] for k in range(n_z // 2)]
    total[1:] = [flip(v, "z", n_z, k + 1) for k, v in enumerate(total[1:])]
    total = (total[0] + total[1]) + (total[2] + total[3])
    stay, leave = total[: pair // 2], total[pair // 2 :]
    summed = stay + flip(leave, "z", n_z, n_z // 2)

    own_grads, head_grads = call(
        grad_rows_body,
        (sds((lists, width)), sds((width, lists), bf16)),
        "grad_rows",
        scratch=(pltpu.VMEM((width, samples), f32),),
        n_in=9, smem=1, flops=2 * 10**9, nbytes=8 * 10**6,
    )(where, targets, grad_sum, grad_out, slope, up, down, normed_in, inv_in)
    returned = lax.all_to_all(head_grads.reshape(toks, head, lists), ("tok", "core"), 0, 0, tiled=True)
    list_grads = call(
        list_body, sds((groups, 2 * capacity, width), bf16), "lists", n_in=2, flops=10**6, nbytes=10**6
    )(own_grads, returned.reshape(width, lists))
    back = lax.all_to_all(list_grads, ("x", "z", "core"), 0, 0, tiled=True)
    new_table, new_accum = call(
        update_body,
        (sds(row_table.shape), sds(row_accum.shape)),
        "update",
        n_in=7, smem=1, flops=10**9, nbytes=3 * 10**6,
    )(step_now, row_table, row_accum, last_step, ids, row_counts[:, 0], back)

    summed = jnp.concatenate([summed[: 2 * third], summed[2 * third :]], axis=1)
    low, high = summed[:third], summed[third:]
    stay, leave = jnp.where(core == 0, low, high), jnp.where(core == 0, high, low)
    come = flip(leave, "core", 2, 1)
    grad_down = jnp.where(core == 0, jnp.stack([stay, come], axis=1), jnp.stack([come, stay], axis=1))
    logits = jnp.where(core == 0, logits[0, :batch], logits[0, batch:])
    return (new_table, new_accum, grad_down, logits)


def solution(mesh):
    devices = mesh.devices.reshape(4, 4, 8, 2)
    wide = Mesh(devices, ("tok", "x", "z", "core"))
    smp = ("x", "z", "core")
    return jax.shard_map(
        on_device,
        mesh=wide,
        in_specs=(
            P("tok", smp, None),
            P("tok", smp),
            P("tok", smp),
            P(),
            P("tok", smp, None, None),
            P("tok", smp, None),
            P(None, smp),
            P(smp),
            P(smp, "tok", None),
            P(smp, "tok", None),
            P("tok", None),
        ),
        out_specs=(P("tok", smp, None), P("tok", smp), P(smp, "tok", None), P(smp)),
        check_vma=False,
    )
```

profile of v0, /device:TPU:2, one launch (start us, length us, event | category | flops | bytes accessed | tf_op | source)
XLA Modules:
  0.0 173.1 jit_solution(3791910323620970274)
XLA Ops:
  4.2 2.0 %collective-permute-start.2 = (bf16[24,1536]{1,0:T(8,128)(2,1)S(1)}, bf16[24,1536]{1,0:T(8,128)(2,1)S(1)}, u32[]{:S(2)}, u32[]{:S(2)}) collective-permute-start(bf16[24,1536]{1,0:T(8,128)(2,1)S(1)} %pad_maximum_fusion.2), channel_id=1, source_target_pairs={{0,2},{2,4},{4,6},{6,8},{8,10},{10,12},{12,14},{14,0},{1,3},{3,5},... | collective-permute-start | bytes 221192 | tf_op jit(solution)/shard_map/ppermute | solution.py:276
  6.2 4.0 %collective-permute-start.3 = (bf16[24,1536]{1,0:T(8,128)(2,1)S(1)}, bf16[24,1536]{1,0:T(8,128)(2,1)S(1)}, u32[]{:S(2)}, u32[]{:S(2)}) collective-permute-start(bf16[24,1536]{1,0:T(8,128)(2,1)S(1)} %pad_maximum_fusion.2), channel_id=1, source_target_pairs={{0,14},{2,0},{4,2},{6,4},{8,6},{10,8},{12,10},{14,12},{1,15},{3,1}... | collective-permute-start | bytes 221192 | tf_op jit(solution)/shard_map/ppermute | solution.py:276
  10.3 1.1 copy-done.21
  12.8 1.5 shard_map.246
  15.2 9.5 %all-to-all-start = ((f16[64,4,384]{2,1,0:T(4,128)(2,1)}), f16[64,4,384]{2,1,0:T(4,128)(2,1)S(1)}, u32[]{:S(2)}, u32[]{:S(2)}) async-start(f16[64,4,384]{2,1,0:T(4,128)(2,1)} %reshape.59), calls=%async_computation | async-start | bytes 393216 | tf_op jit(solution)/shard_map/all_to_all | solution.py:335
  24.8 3.4 %collective-permute-start.4 = (bf16[72,1536]{1,0:T(8,128)(2,1)S(1)}, bf16[72,1536]{1,0:T(8,128)(2,1)S(1)}, u32[]{:S(2)}, u32[]{:S(2)}) collective-permute-start(bf16[72,1536]{1,0:T(8,128)(2,1)S(1)} %pad_maximum_fusion), channel_id=1, source_target_pairs={{0,6},{2,8},{4,10},{6,12},{8,14},{10,0},{12,2},{14,4},{1,7},{3,9},... | collective-permute-start | bytes 663560 | tf_op jit(solution)/shard_map/ppermute | solution.py:276
  28.2 1.8 %collective-permute-start.5 = (bf16[48,1536]{1,0:T(8,128)(2,1)S(1)}, bf16[48,1536]{1,0:T(8,128)(2,1)S(1)}, u32[]{:S(2)}, u32[]{:S(2)}) collective-permute-start(bf16[48,1536]{1,0:T(8,128)(2,1)S(1)} %pad_maximum_fusion.1), channel_id=1, source_target_pairs={{0,10},{2,12},{4,14},{6,0},{8,2},{10,4},{12,6},{14,8},{1,11},{3,13... | collective-permute-start | bytes 442376 | tf_op jit(solution)/shard_map/ppermute | solution.py:276
  30.1 8.6 %collective-permute-done.5 = bf16[48,1536]{1,0:T(8,128)(2,1)S(1)} collective-permute-done((bf16[48,1536]{1,0:T(8,128)(2,1)S(1)}, bf16[48,1536]{1,0:T(8,128)(2,1)S(1)}, u32[]{:S(2)}, u32[]{:S(2)}) %collective-permute-start.5) | collective-permute-done | bytes 147488 | tf_op jit(solution)/shard_map/ppermute | solution.py:276
  38.6 8.8 %collective-permute-done.4 = bf16[72,1536]{1,0:T(8,128)(2,1)S(1)} collective-permute-done((bf16[72,1536]{1,0:T(8,128)(2,1)S(1)}, bf16[72,1536]{1,0:T(8,128)(2,1)S(1)}, u32[]{:S(2)}, u32[]{:S(2)}) %collective-permute-start.4) | collective-permute-done | bytes 221216 | tf_op jit(solution)/shard_map/ppermute | solution.py:276
  47.8 1.7 collective-permute-start.6
  54.1 4.5 %all-to-all-start.1 = ((f16[8,48,256]{2,1,0:T(8,128)(2,1)}), f16[8,48,256]{2,1,0:T(8,128)(2,1)S(1)}, u32[]{:S(2)}, u32[]{:S(2)}) async-start(f16[8,48,256]{2,1,0:T(8,128)(2,1)} %bitcast.8), calls=%async_computation.1 | async-start | bytes 393216 | tf_op jit(solution)/shard_map/all_to_all | solution.py:337
  58.6 3.4 %collective-permute-done.6.xp_ref = bf16[192,1536]{1,0:T(8,128)(2,1)S(1)} collective-permute-done((bf16[192,1536]{1,0:T(8,128)(2,1)S(1)}, bf16[192,1536]{1,0:T(8,128)(2,1)S(1)}, u32[]{:S(2)}, u32[]{:S(2)}) %collective-permute-start.6) | collective-permute-done | bytes 589856 | tf_op jit(solution)/shard_map/ppermute | solution.py:276
  62.0 1.6 collective-permute-start.8
  64.4 1.0 bitcast_convert_fusion.1.own_ref
  65.4 3.6 %collective-permute-done.8.xa_ref = bf16[96,1536]{1,0:T(8,128)(2,1)S(1)} collective-permute-done((bf16[96,1536]{1,0:T(8,128)(2,1)S(1)}, bf16[96,1536]{1,0:T(8,128)(2,1)S(1)}, u32[]{:S(2)}, u32[]{:S(2)}) %collective-permute-start.8) | collective-permute-done | bytes 294944 | tf_op jit(solution)/shard_map/ppermute | solution.py:276
  69.8 0.9 collective-permute-done.9.xb_ref
  71.4 1.1 copy-done.7
  72.5 0.9 copy-done.8
  73.4 1.1 copy-done.12
  74.5 1.1 copy-done.14
  77.0 1.0 copy-done.24
  78.0 1.0 copy-done.26
  78.9 10.8 %shard_map.247 = (f32[384,512]{1,0:T(8,128)S(1)}, f32[1,512]{1,0:T(1,128)S(1)}, bf16[512,1536]{1,0:T(8,128)(2,1)S(1)}, f32[512,1536]{1,0:T(8,128)S(1)}, f32[384,...) custom-call(s32[1]{0:T(128)} %bitcast.4.where_ref, ...), custom_call_target="tpu_custom_call" | custom-call | flops 4000000000 | bytes 10000000 | tf_op jit(solution)/shard_map/pallas_call | solution.py:370
  89.7 1.0 copy-done
  90.7 1.0 copy-done.2
  91.8 0.9 copy-done.4
  93.3 1.2 copy-done.33
  98.4 1.6 collective-permute-start.11
  100.0 2.9 %collective-permute-start.12 = (f32[1,512]{1,0:T(1,128)S(1)}, f32[1,512]{1,0:T(1,128)S(1)}, u32[]{:S(2)}, u32[]{:S(2)}) collective-permute-start(f32[1,512]{1,0:T(1,128)S(1)} %add.107), channel_id=1, source_target_pairs={{0,128},{64,192},{128,0},{192,64},{1,129},{65,193},{129,1},{193,65... | collective-permute-start | bytes 6152 | tf_op jit(solution)/shard_map/ppermute | solution.py:280
  103.8 1.2 collective-permute-done.12
  105.1 2.6 %collective-permute-done.13 = f32[1,512]{1,0:T(1,128)S(1)} collective-permute-done((f32[1,512]{1,0:T(1,128)S(1)}, f32[1,512]{1,0:T(1,128)S(1)}, u32[]{:S(2)}, u32[]{:S(2)}) %collective-permute-start.13) | collective-permute-done | bytes 2080 | tf_op jit(solution)/shard_map/ppermute | solution.py:280
  107.7 1.4 copy-done.34
  109.1 3.0 %shard_map.249 = (f32[384,512]{1,0:T(8,128)S(1)}, bf16[512,384]{1,0:T(8,128)(2,1)S(1)}, f32[192,768]{1,0:T(8,128)S(1)}, bf16[192,768]{1,0:T(8,128)(2,1)S(1)}, bf...) custom-call(bf16[2,768,384]{2,1,0:T(8,128)(2,1)S(1)} %shard_map.248.place_ref, ...), custom_call_target="tpu_custom_call" | custom-call | flops 2000000000 | bytes 5000000 | tf_op jit(solution)/shard_map/pallas_call | solution.py:388
  112.2 1.4 collective-permute-start.14
  113.5 2.8 %collective-permute-start.15 = (bf16[192,768]{1,0:T(8,128)(2,1)S(1)}, bf16[192,768]{1,0:T(8,128)(2,1)S(1)}, u32[]{:S(2)}, u32[]{:S(2)}) collective-permute-start(bf16[192,768]{1,0:T(8,128)(2,1)S(1)} %get-tuple-element.42), channel_id=1, source_target_pairs={{0,32},{16,48},{32,0},{48,16},{1,33},{17,49},{33,1},{49,17},{2,34}... | collective-permute-start | bytes 884744 | tf_op jit(solution)/shard_map/ppermute | solution.py:276
  116.4 2.0 %collective-permute-start.16 = (bf16[192,768]{1,0:T(8,128)(2,1)S(1)}, bf16[192,768]{1,0:T(8,128)(2,1)S(1)}, u32[]{:S(2)}, u32[]{:S(2)}) collective-permute-start(bf16[192,768]{1,0:T(8,128)(2,1)S(1)} %get-tuple-element.43), channel_id=1, source_target_pairs={{0,48},{16,0},{32,16},{48,32},{1,49},{17,1},{33,17},{49,33},{2,50}... | collective-permute-start | bytes 884744 | tf_op jit(solution)/shard_map/ppermute | solution.py:276
  118.3 3.8 %collective-permute-done.14 = bf16[192,768]{1,0:T(8,128)(2,1)S(1)} collective-permute-done((bf16[192,768]{1,0:T(8,128)(2,1)S(1)}, bf16[192,768]{1,0:T(8,128)(2,1)S(1)}, u32[]{:S(2)}, u32[]{:S(2)}) %collective-permute-start.14) | collective-permute-done | bytes 294944 | tf_op jit(solution)/shard_map/ppermute | solution.py:276
  122.2 2.8 %collective-permute-done.15 = bf16[192,768]{1,0:T(8,128)(2,1)S(1)} collective-permute-done((bf16[192,768]{1,0:T(8,128)(2,1)S(1)}, bf16[192,768]{1,0:T(8,128)(2,1)S(1)}, u32[]{:S(2)}, u32[]{:S(2)}) %collective-permute-start.15) | collective-permute-done | bytes 294944 | tf_op jit(solution)/shard_map/ppermute | solution.py:276
  125.0 3.8 %collective-permute-done.16 = bf16[192,768]{1,0:T(8,128)(2,1)S(1)} collective-permute-done((bf16[192,768]{1,0:T(8,128)(2,1)S(1)}, bf16[192,768]{1,0:T(8,128)(2,1)S(1)}, u32[]{:S(2)}, u32[]{:S(2)}) %collective-permute-start.16) | collective-permute-done | bytes 294944 | tf_op jit(solution)/shard_map/ppermute | solution.py:276
  129.7 1.5 collective-permute-start.18
  131.3 2.8 %collective-permute-start.19 = (f32[48,768]{1,0:T(8,128)}, f32[48,768]{1,0:T(8,128)}, u32[]{:S(2)}, u32[]{:S(2)}) collective-permute-start(f32[48,768]{1,0:T(8,128)} %get-tuple-element.56), channel_id=1, source_target_pairs={{0,6},{2,4},{4,2},{6,0},{8,14},{10,12},{12,10},{14,8},{1,7},{3,5},... | collective-permute-start | bytes 442376 | tf_op jit(solution)/shard_map/ppermute | solution.py:280
  134.1 5.9 %shard_map.250 = (f32[256,384]{1,0:T(8,128)S(1)}, bf16[384,256]{1,0:T(8,128)(2,1)S(1)}) custom-call(s32[1]{0:T(128)} %bitcast.4.where_ref, s32[8,512]{1,0:T(8,128)S(1)} %get-tuple-element.24.target_ref, f32[384,512]{1,0:T(8,128)S(1)} %get-tuple-element.29.grad_sum_ref, bf16[512,384]{1,0:T(8,128)(2,1)S(1)} %get-tuple-element.30.grad_out_ref, ...), custom_call_target="tpu_custom_call" | custom-call | flops 2000000000 | bytes 8000000 | tf_op jit(solution)/shard_map/pallas_call | solution.py:404
  140.7 3.4 %all-to-all-start.2 = ((bf16[8,48,256]{2,1,0:T(8,128)(2,1)}), bf16[8,48,256]{2,1,0:T(8,128)(2,1)S(1)}, u32[]{:S(2)}, u32[]{:S(2)}) async-start(bf16[8,48,256]{2,1,0:T(8,128)(2,1)} %bitcast.28), calls=%async_computation.2 | async-start | bytes 393216 | tf_op jit(solution)/shard_map/all_to_all | solution.py:411
  144.2 1.2 fusion
  145.4 5.5 %collective-permute-start.20 = (f32[24,768]{1,0:T(8,128)S(1)}, f32[24,768]{1,0:T(8,128)S(1)}, u32[]{:S(2)}, u32[]{:S(2)}) collective-permute-start(f32[24,768]{1,0:T(8,128)S(1)} %slice.88), channel_id=1, source_target_pairs={{0,8},{2,10},{4,12},{6,14},{8,0},{10,2},{12,4},{14,6},{1,9},{3,11}... | collective-permute-start | bytes 221192 | tf_op jit(solution)/shard_map/ppermute | solution.py:280
  151.7 8.9 %all-to-all-start.3 = ((bf16[64,4,384]{2,1,0:T(4,128)(2,1)}), bf16[64,4,384]{2,1,0:T(4,128)(2,1)S(1)}, u32[]{:S(2)}, u32[]{:S(2)}) async-start(bf16[64,4,384]{2,1,0:T(4,128)(2,1)} %shard_map.251), calls=%async_computation.3 | async-start | bytes 393216 | tf_op jit(solution)/shard_map/all_to_all | solution.py:415
  162.7 8.2 %all-to-all-done.3.back_ref = bf16[64,4,384]{2,1,0:T(4,128)(2,1)S(1)} async-done(((bf16[64,4,384]{2,1,0:T(4,128)(2,1)}), bf16[64,4,384]{2,1,0:T(4,128)(2,1)S(1)}, u32[]{:S(2)}, u32[]{:S(2)}) %all-to-all-start.3) | async-done | bytes 196640 | tf_op jit(solution)/shard_map/all_to_all | solution.py:415
  170.9 2.2 %shard_map.252 = (f32[2,256,384]{2,1,0:T(8,128)}, f32[2,256]{1,0:T(2,128)}) custom-call(s32[1]{0:T(128)S(6)} %copy.46.step_ref, f32[2,256,384]{2,1,0:T(8,128)S(1)} %copy-done.22, f32[2,256]{1,0:T(2,128)S(1)} %copy-done.27, s32[2,256]{1,0:T(2,128)S(1)} %copy-done.29, s32[4,64]{1,0:T(4,128)S(1)} %bitcast.30, s32[2,64]{1,0:T(2,128)S(1)} %bitcast.31, ...), custom_call_target="tpu_custom_call" | custom-call | flops 1000000000 | bytes 3000000 | tf_op jit(solution)/shard_map/pallas_call | solution.py:416
  (167 shorter events, 23.9 us)
Async XLA Ops:
  2.2 2.0 %collective-permute-start.1 = (bf16[12,1536]{1,0:T(8,128)(2,1)S(1)}, bf16[12,1536]{1,0:T(8,128)(2,1)S(1)}, u32[]{:S(2)}, u32[]{:S(2)}) collective-permute-start(bf16[12,1536]{1,0:T(8,128)(2,1)S(1)} %get-tuple-element.62), channel_id=1, source_target_pairs={{0,1},{1,0},{2,3},{3,2},{4,5},{5,4},{6,7},{7,6},{8,9},{9,8},{10,11... | collective-permute-start | bytes 110600 | tf_op jit(solution)/shard_map/ppermute | solution.py:280
  3.1 49.5 %collective-permute-start = (s32[16,256]{1,0:T(8,128)S(1)}, s32[16,256]{1,0:T(8,128)S(1)}, u32[]{:S(2)}, u32[]{:S(2)}) collective-permute-start(s32[16,256]{1,0:T(8,128)S(1)} %pad_add_fusion), channel_id=1, source_target_pairs={{0,1},{1,0},{2,3},{3,2},{4,5},{5,4},{6,7},{7,6},{8,9},{9,8},{10,11... | collective-permute-start | bytes 49160 | tf_op jit(solution)/shard_map/ppermute | solution.py:280
  4.2 20.5 %collective-permute-start.2 = (bf16[24,1536]{1,0:T(8,128)(2,1)S(1)}, bf16[24,1536]{1,0:T(8,128)(2,1)S(1)}, u32[]{:S(2)}, u32[]{:S(2)}) collective-permute-start(bf16[24,1536]{1,0:T(8,128)(2,1)S(1)} %pad_maximum_fusion.2), channel_id=1, source_target_pairs={{0,2},{2,4},{4,6},{6,8},{8,10},{10,12},{12,14},{14,0},{1,3},{3,5},... | collective-permute-start | bytes 221192 | tf_op jit(solution)/shard_map/ppermute | solution.py:276
  6.2 18.5 %collective-permute-start.3 = (bf16[24,1536]{1,0:T(8,128)(2,1)S(1)}, bf16[24,1536]{1,0:T(8,128)(2,1)S(1)}, u32[]{:S(2)}, u32[]{:S(2)}) collective-permute-start(bf16[24,1536]{1,0:T(8,128)(2,1)S(1)} %pad_maximum_fusion.2), channel_id=1, source_target_pairs={{0,14},{2,0},{4,2},{6,4},{8,6},{10,8},{12,10},{14,12},{1,15},{3,1}... | collective-permute-start | bytes 221192 | tf_op jit(solution)/shard_map/ppermute | solution.py:276
  14.3 15.7 %copy-start.47 = (s32[768]{0:T(1024)S(1)}, s32[768]{0:T(1024)}, u32[]{:S(2)}) copy-start(s32[768]{0:T(1024)} %constant.86.clone) | copy-start | bytes 9220
  14.3 15.7 %copy-start.48 = (s32[768]{0:T(1024)S(1)}, s32[768]{0:T(1024)}, u32[]{:S(2)}) copy-start(s32[768]{0:T(1024)} %constant.87.clone) | copy-start | bytes 9220
  14.3 15.7 %copy-start.49 = (s32[768]{0:T(1024)S(1)}, s32[768]{0:T(1024)}, u32[]{:S(2)}) copy-start(s32[768]{0:T(1024)} %constant.88.clone) | copy-start | bytes 9220
  14.3 15.7 %copy-start.50 = (s32[768]{0:T(1024)S(1)}, s32[768]{0:T(1024)}, u32[]{:S(2)}) copy-start(s32[768]{0:T(1024)} %constant.89.clone) | copy-start | bytes 9220
  15.2 34.7 %copy-start.44 = (s32[768]{0:T(1024)S(1)}, s32[768]{0:T(1024)}, u32[]{:S(2)}) copy-start(s32[768]{0:T(1024)} %constant.93.clone) | copy-start | bytes 9220
  15.2 34.7 %copy-start.45 = (s32[768]{0:T(1024)S(1)}, s32[768]{0:T(1024)}, u32[]{:S(2)}) copy-start(s32[768]{0:T(1024)} %constant.94.clone) | copy-start | bytes 9220
  15.2 34.7 %copy-start.46 = (s32[768]{0:T(1024)S(1)}, s32[768]{0:T(1024)}, u32[]{:S(2)}) copy-start(s32[768]{0:T(1024)} %constant.95.clone) | copy-start | bytes 9220
  15.2 34.7 %copy-start.53 = (pred[768]{0:T(1024)(128)(4,1)S(1)}, pred[768]{0:T(1024)(128)(4,1)}, u32[]{:S(2)}) copy-start(pred[768]{0:T(1024)(128)(4,1)} %constant.96.clone) | copy-start | bytes 2308
  15.2 34.7 %copy-start.54 = (pred[768]{0:T(1024)(128)(4,1)S(1)}, pred[768]{0:T(1024)(128)(4,1)}, u32[]{:S(2)}) copy-start(pred[768]{0:T(1024)(128)(4,1)} %constant.97.clone) | copy-start | bytes 2308
  15.2 34.7 %copy-start.52 = (f32[2,384]{1,0:T(2,128)S(1)}, f32[2,384]{1,0:T(2,128)}, u32[]{:S(2)}) copy-start(f32[2,384]{1,0:T(2,128)} %param.33) | copy-start | bytes 9220
  15.2 38.0 %all-to-all-start = ((f16[64,4,384]{2,1,0:T(4,128)(2,1)}), f16[64,4,384]{2,1,0:T(4,128)(2,1)S(1)}, u32[]{:S(2)}, u32[]{:S(2)}) async-start(f16[64,4,384]{2,1,0:T(4,128)(2,1)} %reshape.59), calls=%async_computation | async-start | bytes 393216 | tf_op jit(solution)/shard_map/all_to_all | solution.py:335
  24.7 27.9 %copy-start.40 = (s32[8,256]{1,0:T(8,128)S(1)}, s32[8,256]{1,0:T(8,128)}, u32[]{:S(2)}) copy-start(s32[8,256]{1,0:T(8,128)} %param.29) | copy-start | bytes 24580
  24.7 27.9 %copy-start.43 = (s32[256]{0:T(256)S(1)}, s32[256]{0:T(256)}, u32[]{:S(2)}) copy-start(s32[256]{0:T(256)} %param.30) | copy-start | bytes 3076
  24.8 22.6 %collective-permute-start.4 = (bf16[72,1536]{1,0:T(8,128)(2,1)S(1)}, bf16[72,1536]{1,0:T(8,128)(2,1)S(1)}, u32[]{:S(2)}, u32[]{:S(2)}) collective-permute-start(bf16[72,1536]{1,0:T(8,128)(2,1)S(1)} %pad_maximum_fusion), channel_id=1, source_target_pairs={{0,6},{2,8},{4,10},{6,12},{8,14},{10,0},{12,2},{14,4},{1,7},{3,9},... | collective-permute-start | bytes 663560 | tf_op jit(solution)/shard_map/ppermute | solution.py:276
  28.2 10.5 %collective-permute-start.5 = (bf16[48,1536]{1,0:T(8,128)(2,1)S(1)}, bf16[48,1536]{1,0:T(8,128)(2,1)S(1)}, u32[]{:S(2)}, u32[]{:S(2)}) collective-permute-start(bf16[48,1536]{1,0:T(8,128)(2,1)S(1)} %pad_maximum_fusion.1), channel_id=1, source_target_pairs={{0,10},{2,12},{4,14},{6,0},{8,2},{10,4},{12,6},{14,8},{1,11},{3,13... | collective-permute-start | bytes 442376 | tf_op jit(solution)/shard_map/ppermute | solution.py:276
  47.8 15.9 %copy-start.6 = (bf16[192,1536]{1,0:T(8,128)(2,1)}, bf16[192,1536]{1,0:T(8,128)(2,1)S(1)}, u32[]{:S(2)}) copy-start(bf16[192,1536]{1,0:T(8,128)(2,1)S(1)} %concatenate.37.z_ref) | copy-start | bytes 1769476
  47.8 14.2 %collective-permute-start.6 = (bf16[192,1536]{1,0:T(8,128)(2,1)S(1)}, bf16[192,1536]{1,0:T(8,128)(2,1)S(1)}, u32[]{:S(2)}, u32[]{:S(2)}) collective-permute-start(bf16[192,1536]{1,0:T(8,128)(2,1)S(1)} %concatenate.37.z_ref), channel_id=1, source_target_pairs={{0,16},{16,32},{32,48},{48,0},{1,17},{17,33},{33,49},{49,1},{2,18}... | collective-permute-start | bytes 1769480 | tf_op jit(solution)/shard_map/ppermute | solution.py:276
  49.5 14.2 %collective-permute-start.7 = (bf16[192,1536]{1,0:T(8,128)(2,1)S(1)}, bf16[192,1536]{1,0:T(8,128)(2,1)S(1)}, u32[]{:S(2)}, u32[]{:S(2)}) collective-permute-start(bf16[192,1536]{1,0:T(8,128)(2,1)S(1)} %concatenate.37.z_ref), channel_id=1, source_target_pairs={{0,48},{16,0},{32,16},{48,32},{1,49},{17,1},{33,17},{49,33},{2,50}... | collective-permute-start | bytes 1769480 | tf_op jit(solution)/shard_map/ppermute | solution.py:276
  54.1 11.3 %all-to-all-start.1 = ((f16[8,48,256]{2,1,0:T(8,128)(2,1)}), f16[8,48,256]{2,1,0:T(8,128)(2,1)S(1)}, u32[]{:S(2)}, u32[]{:S(2)}) async-start(f16[8,48,256]{2,1,0:T(8,128)(2,1)} %bitcast.8), calls=%async_computation.1 | async-start | bytes 393216 | tf_op jit(solution)/shard_map/all_to_all | solution.py:337
  62.0 7.0 %collective-permute-start.8 = (bf16[96,1536]{1,0:T(8,128)(2,1)S(1)}, bf16[96,1536]{1,0:T(8,128)(2,1)S(1)}, u32[]{:S(2)}, u32[]{:S(2)}) collective-permute-start(bf16[96,1536]{1,0:T(8,128)(2,1)S(1)} %slice.80), channel_id=1, source_target_pairs={{0,16},{16,32},{32,48},{48,0},{1,17},{17,33},{33,49},{49,1},{2,18}... | collective-permute-start | bytes 884744 | tf_op jit(solution)/shard_map/ppermute | solution.py:276
  63.7 7.0 %collective-permute-start.9 = (bf16[96,1536]{1,0:T(8,128)(2,1)S(1)}, bf16[96,1536]{1,0:T(8,128)(2,1)S(1)}, u32[]{:S(2)}, u32[]{:S(2)}) collective-permute-start(bf16[96,1536]{1,0:T(8,128)(2,1)S(1)} %slice.81), channel_id=1, source_target_pairs={{0,48},{16,0},{32,16},{48,32},{1,49},{17,1},{33,17},{49,33},{2,50}... | collective-permute-start | bytes 884744 | tf_op jit(solution)/shard_map/ppermute | solution.py:276
  78.9 17.0 %copy-start.41 = (s32[768,1]{0,1:T(1,128)S(1)}, s32[768,1]{0,1:T(1,128)}, u32[]{:S(2)}) copy-start(s32[768,1]{0,1:T(1,128)} %stack.35) | copy-start | bytes 9220
  78.9 17.0 %copy-start.42 = (s32[768,1]{0,1:T(1,128)S(1)}, s32[768,1]{0,1:T(1,128)}, u32[]{:S(2)}) copy-start(s32[768,1]{0,1:T(1,128)} %stack.36) | copy-start | bytes 9220
  95.9 1.8 %collective-permute-start.10 = (f32[1,512]{1,0:T(1,128)}, f32[1,512]{1,0:T(1,128)}, u32[]{:S(2)}, u32[]{:S(2)}) collective-permute-start(f32[1,512]{1,0:T(1,128)} %get-tuple-element.25), channel_id=1, source_target_pairs={{0,1},{1,0},{2,3},{3,2},{4,5},{5,4},{6,7},{7,6},{8,9},{9,8},{10,11... | collective-permute-start | bytes 6152 | tf_op jit(solution)/shard_map/ppermute | solution.py:280
  98.4 5.4 %collective-permute-start.11 = (f32[1,512]{1,0:T(1,128)S(1)}, f32[1,512]{1,0:T(1,128)S(1)}, u32[]{:S(2)}, u32[]{:S(2)}) collective-permute-start(f32[1,512]{1,0:T(1,128)S(1)} %add.107), channel_id=1, source_target_pairs={{0,64},{64,0},{128,192},{192,128},{1,65},{65,1},{129,193},{193,129... | collective-permute-start | bytes 6152 | tf_op jit(solution)/shard_map/ppermute | solution.py:280
  100.0 5.1 %collective-permute-start.12 = (f32[1,512]{1,0:T(1,128)S(1)}, f32[1,512]{1,0:T(1,128)S(1)}, u32[]{:S(2)}, u32[]{:S(2)}) collective-permute-start(f32[1,512]{1,0:T(1,128)S(1)} %add.107), channel_id=1, source_target_pairs={{0,128},{64,192},{128,0},{192,64},{1,129},{65,193},{129,1},{193,65... | collective-permute-start | bytes 6152 | tf_op jit(solution)/shard_map/ppermute | solution.py:280
  102.9 4.8 %collective-permute-start.13 = (f32[1,512]{1,0:T(1,128)S(1)}, f32[1,512]{1,0:T(1,128)S(1)}, u32[]{:S(2)}, u32[]{:S(2)}) collective-permute-start(f32[1,512]{1,0:T(1,128)S(1)} %add.107), channel_id=1, source_target_pairs={{0,192},{64,128},{128,64},{192,0},{1,193},{65,129},{129,65},{193,1... | collective-permute-start | bytes 6152 | tf_op jit(solution)/shard_map/ppermute | solution.py:280
  109.1 25.0 %copy-start.5 = (f32[384,512]{1,0:T(8,128)S(1)}, f32[384,512]{1,0:T(8,128)}, u32[]{:S(2)}) copy-start(f32[384,512]{1,0:T(8,128)} %copy-done.4) | copy-start | bytes 2359300
  112.2 10.0 %collective-permute-start.14 = (bf16[192,768]{1,0:T(8,128)(2,1)S(1)}, bf16[192,768]{1,0:T(8,128)(2,1)S(1)}, u32[]{:S(2)}, u32[]{:S(2)}) collective-permute-start(bf16[192,768]{1,0:T(8,128)(2,1)S(1)} %get-tuple-element.41), channel_id=1, source_target_pairs={{0,16},{16,32},{32,48},{48,0},{1,17},{17,33},{33,49},{49,1},{2,18}... | collective-permute-start | bytes 884744 | tf_op jit(solution)/shard_map/ppermute | solution.py:276
  113.5 11.4 %collective-permute-start.15 = (bf16[192,768]{1,0:T(8,128)(2,1)S(1)}, bf16[192,768]{1,0:T(8,128)(2,1)S(1)}, u32[]{:S(2)}, u32[]{:S(2)}) collective-permute-start(bf16[192,768]{1,0:T(8,128)(2,1)S(1)} %get-tuple-element.42), channel_id=1, source_target_pairs={{0,32},{16,48},{32,0},{48,16},{1,33},{17,49},{33,1},{49,17},{2,34}... | collective-permute-start | bytes 884744 | tf_op jit(solution)/shard_map/ppermute | solution.py:276
  116.4 12.4 %collective-permute-start.16 = (bf16[192,768]{1,0:T(8,128)(2,1)S(1)}, bf16[192,768]{1,0:T(8,128)(2,1)S(1)}, u32[]{:S(2)}, u32[]{:S(2)}) collective-permute-start(bf16[192,768]{1,0:T(8,128)(2,1)S(1)} %get-tuple-element.43), channel_id=1, source_target_pairs={{0,48},{16,0},{32,16},{48,32},{1,49},{17,1},{33,17},{49,33},{2,50}... | collective-permute-start | bytes 884744 | tf_op jit(solution)/shard_map/ppermute | solution.py:276
  129.7 14.4 %collective-permute-start.17 = (f32[48,768]{1,0:T(8,128)}, f32[48,768]{1,0:T(8,128)}, u32[]{:S(2)}, u32[]{:S(2)}) collective-permute-start(f32[48,768]{1,0:T(8,128)} %get-tuple-element.58), channel_id=1, source_target_pairs={{0,2},{2,0},{4,6},{6,4},{8,10},{10,8},{12,14},{14,12},{1,3},{3,1},... | collective-permute-start | bytes 442376 | tf_op jit(solution)/shard_map/ppermute | solution.py:280
  129.7 14.4 %collective-permute-start.18 = (f32[48,768]{1,0:T(8,128)}, f32[48,768]{1,0:T(8,128)}, u32[]{:S(2)}, u32[]{:S(2)}) collective-permute-start(f32[48,768]{1,0:T(8,128)} %get-tuple-element.57), channel_id=1, source_target_pairs={{0,4},{2,6},{4,0},{6,2},{8,12},{10,14},{12,8},{14,10},{1,5},{3,7},... | collective-permute-start | bytes 442376 | tf_op jit(solution)/shard_map/ppermute | solution.py:280
  131.3 12.9 %collective-permute-start.19 = (f32[48,768]{1,0:T(8,128)}, f32[48,768]{1,0:T(8,128)}, u32[]{:S(2)}, u32[]{:S(2)}) collective-permute-start(f32[48,768]{1,0:T(8,128)} %get-tuple-element.56), channel_id=1, source_target_pairs={{0,6},{2,4},{4,2},{6,0},{8,14},{10,12},{12,10},{14,8},{1,7},{3,5},... | collective-permute-start | bytes 442376 | tf_op jit(solution)/shard_map/ppermute | solution.py:280
  140.7 10.2 %all-to-all-start.2 = ((bf16[8,48,256]{2,1,0:T(8,128)(2,1)}), bf16[8,48,256]{2,1,0:T(8,128)(2,1)S(1)}, u32[]{:S(2)}, u32[]{:S(2)}) async-start(bf16[8,48,256]{2,1,0:T(8,128)(2,1)} %bitcast.28), calls=%async_computation.2 | async-start | bytes 393216 | tf_op jit(solution)/shard_map/all_to_all | solution.py:411
  144.1 16.7 %copy-start.17 = (f32[1,512]{1,0:T(1,128)S(1)}, f32[1,512]{1,0:T(1,128)}, u32[]{:S(2)}) copy-start(f32[1,512]{1,0:T(1,128)} %copy-done.16) | copy-start | bytes 6148
  145.3 25.6 %copy-start.22 = (f32[2,256,384]{2,1,0:T(8,128)S(1)}, f32[2,256,384]{2,1,0:T(8,128)}, u32[]{:S(2)}) copy-start(f32[2,256,384]{2,1,0:T(8,128)} %table_ref.1) | copy-start | bytes 2359300
  145.3 25.6 %copy-start.27 = (f32[2,256]{1,0:T(2,128)S(1)}, f32[2,256]{1,0:T(2,128)}, u32[]{:S(2)}) copy-start(f32[2,256]{1,0:T(2,128)} %accum_ref.1) | copy-start | bytes 6148
  145.4 25.6 %copy-start.29 = (s32[2,256]{1,0:T(2,128)S(1)}, s32[2,256]{1,0:T(2,128)}, u32[]{:S(2)}) copy-start(s32[2,256]{1,0:T(2,128)} %last_ref.1) | copy-start | bytes 6148
  145.4 25.6 %copy-start.31 = (s32[2,1,64,2]{2,3,1,0:T(2,128)S(1)}, s32[2,1,64,2]{2,3,1,0:T(2,128)}, u32[]{:S(2)}) copy-start(s32[2,1,64,2]{2,3,1,0:T(2,128)} %param.27) | copy-start | bytes 3076
  145.4 25.6 %copy-start.32 = (s32[2,1,64]{2,1,0:T(1,128)S(1)}, s32[2,1,64]{2,1,0:T(1,128)}, u32[]{:S(2)}) copy-start(s32[2,1,64]{2,1,0:T(1,128)} %param.28) | copy-start | bytes 1540
  145.4 15.2 %collective-permute-start.20 = (f32[24,768]{1,0:T(8,128)S(1)}, f32[24,768]{1,0:T(8,128)S(1)}, u32[]{:S(2)}, u32[]{:S(2)}) collective-permute-start(f32[24,768]{1,0:T(8,128)S(1)} %slice.88), channel_id=1, source_target_pairs={{0,8},{2,10},{4,12},{6,14},{8,0},{10,2},{12,4},{14,6},{1,9},{3,11}... | collective-permute-start | bytes 221192 | tf_op jit(solution)/shard_map/ppermute | solution.py:280
  151.7 19.2 %all-to-all-start.3 = ((bf16[64,4,384]{2,1,0:T(4,128)(2,1)}), bf16[64,4,384]{2,1,0:T(4,128)(2,1)S(1)}, u32[]{:S(2)}, u32[]{:S(2)}) async-start(bf16[64,4,384]{2,1,0:T(4,128)(2,1)} %shard_map.251), calls=%async_computation.3 | async-start | bytes 393216 | tf_op jit(solution)/shard_map/all_to_all | solution.py:415
  160.6 1.3 collective-permute-start.21
  (35 other events, 139.6 us)
where the time goes:
time: 176 us; the launch traced here: 173 us
  starting transfers between devices  63.3 us (36%)
  waiting for transfers between devices  48.4 us (28%)
  local copies, waits for them, and re-layouts  27.8 us (16%)
  Pallas kernels  24.5 us (14%)
  other arithmetic  7.07 us (4%)
  between operations  1.97 us (1%)
    ppermute x11, waiting for transfers between devices, ring(): lax.ppermute(value, axis, [(i, (i + shift) % size) for i in range(size)])  35.8 us
    unnamed x117, local copies, waits for them, and re-layouts  22.1 us
    ppermute x11, starting transfers between devices, ring(): lax.ppermute(value, axis, [(i, (i + shift) % size) for i in range(size)])  21.8 us
    ppermute x11, starting transfers between devices, flip(): return lax.ppermute(value, axis, [(i, i ^ bit) for i in range(size)])  15.3 us
    pallas_call x1, Pallas kernels, on_device(): call(forward_body, (sds((width, samples)), sds((1, samples)), sds(full, b...  10.8 us
    all_to_all x1, starting transfers between devices, on_device(): got = lax.all_to_all(sent, ('x', 'z', 'core'), 0, 0, tiled=True)  9.46 us
    all_to_all x1, starting transfers between devices, on_device(): back = lax.all_to_all(list_grads, ('x', 'z', 'core'), 0, 0, tiled=True)  8.86 us
    all_to_all x1, waiting for transfers between devices, on_device(): back = lax.all_to_all(list_grads, ('x', 'z', 'core'), 0, 0, tiled=True)  8.24 us
  transfers between devices with their start and end apart: 26, of which 12 were waited for; matrix products, arithmetic and copies ran while one was open for 7% of the time, Pallas kernels for 5%

commit v1 on v0

--- a/solution.py
+++ b/solution.py
@@ -118,7 +118,7 @@
 def forward_body(
     where_ref, own_ref, heads_ref, slots_ref, head_ref, order_ref, z_ref, xp_ref, xm_ref, xa_ref, xb_ref,
     normed_in_ref, inv_in_ref, active_ref, slope_ref, normed_out_ref, inv_out_ref, logit_ref, up_ref, down_ref,
-    target_ref, all_ref, total_ref, input_ref, choice_ref,
+    target_ref, all_ref, total_ref, input_ref,
 ):
     start = 0
     for ref in (z_ref, xp_ref, xm_ref, xa_ref, xb_ref):
@@ -129,8 +129,8 @@
     toks = slots_ref.shape[0] // 2
     head = width // toks
     rows, hidden = all_ref.shape
-    for k in range(2):
-        choice_ref[k * width : (k + 1) * width] = (iota((width, rows), 0) == order_ref[k : k + 1, :]).astype(bf16)
+    order_up = (iota((width, rows), 0) == order_ref[0:1, :]).astype(bf16)
+    order_down = (iota((width, rows), 0) == order_ref[1:2, :]).astype(bf16)
     targets = list_targets(slots_ref[0:toks, :], samples // 2)
     target_ref[...] = targets
     row = iota((lists, samples), 0)
@@ -153,8 +153,9 @@
     @pl.loop(0, hidden // chunk)
     def _(i):
         cols = pl.ds(pl.multiple_of(i * chunk, chunk), chunk)
-        both = dot(choice_ref[...], all_ref[:, cols]).astype(bf16)
-        up, down = both[:width], both[width:]
+        block = all_ref[:, cols]
+        up = dot(order_up, block).astype(bf16)
+        down = dot(order_down, block).astype(bf16)
         up_ref[:, cols] = up
         down_ref[:, cols] = down
         pre = dot(input_ref[...], up)
@@ -182,10 +183,12 @@
 
 
 def grad_down_body(
-    place_ref, logit_ref, label_ref, head_ref, normed_out_ref, inv_out_ref, active_ref,
+    place_ref, logit_ref, slots_ref, head_ref, normed_out_ref, inv_out_ref, active_ref,
     grad_sum_ref, grad_out_ref, kept_ref, next_ref, far_ref, last_ref, padded_ref,
 ):
-    dlogit = jax.nn.sigmoid(logit_ref[...]) - label_ref[...]
+    toks = slots_ref.shape[0] // 2
+    labels = slots_ref[toks : toks + 1, :].astype(f32)
+    dlogit = jax.nn.sigmoid(logit_ref[...]) - labels
     grad = norm_back(dlogit * head_ref[...], normed_out_ref[...], inv_out_ref[...])
     grad_sum_ref[...] = grad
     rounded = grad.astype(bf16)
@@ -346,7 +349,6 @@
     mine = jnp.concatenate([sample_slots, labels[None], jnp.zeros((toks - 1, batch), i32)], axis=0)
     theirs = flip(mine, "core", 2, 1)
     slots = jnp.where(core == 0, jnp.concatenate([mine, theirs], axis=1), jnp.concatenate([theirs, mine], axis=1))
-    label_row = slots[toks : toks + 1].astype(f32)
     before, after = ring(piece, "z", n_z, 1), ring(piece, "z", n_z, -1)
     pair = jnp.concatenate([before, piece], axis=0)
     three = jnp.concatenate([before, piece, after], axis=0)
@@ -376,9 +378,8 @@
         "forward",
         scratch=(
             pltpu.VMEM((4 * part, hidden), bf16), pltpu.VMEM((width, samples), f32), pltpu.VMEM((samples, width), bf16),
-            pltpu.VMEM((2 * width, 4 * part), bf16),
         ),
-        n_in=11, smem=1, flops=4 * 10**9, nbytes=10**7, room=24,
+        n_in=11, smem=1, flops=4 * 10**9, nbytes=10**7, room=40,
     )(where, own, heads, slots, head_weight, order, line, x_before, x_after, far_a, far_b)
     logits = partial + flip(partial, "core", 2, 1)
     there = [flip(logits, "tok", n_tok, k) for k in (1, 2, 3)]
@@ -391,7 +392,7 @@
         "grad_down",
         scratch=(pltpu.VMEM((2, n_x * lines, samples), bf16),),
         n_in=7, flops=2 * 10**9, nbytes=5 * 10**6,
-    )(place, logits, label_row, head_weight, normed_out, inv_out, active)
+    )(place, logits, slots, head_weight, normed_out, inv_out, active)
     come = [ring(v, "x", n_x, k + 1) for k, v in enumerate(away)]
     pair = 8 * third
     total = kept + sum(v.astype(f32) for v in come)

time: 176 us -> 162 us (0.920)
  waiting for transfers between devices: 48.4 us -> 41.7 us
  local copies, waits for them, and re-layouts: 27.8 us -> 23.1 us
    ppermute x11, waiting for transfers between devices: 35.8 us -> 19.3 us  [ring(): lax.ppermute(value, axis, [(i, (i + shift) % size) for i in range(size)])]
    all_to_all x1, waiting for transfers between devices: 0.01 us -> 4.98 us  [on_device(): got = lax.all_to_all(sent, ('x', 'z', 'core'), 0, 0, tiled=True)]
    unnamed x117 -> x115, local copies, waits for them, and re-layouts: 22.1 us -> 18.5 us
    ppermute x11, waiting for transfers between devices: 4.41 us -> 7.59 us  [flip(): return lax.ppermute(value, axis, [(i, i ^ bit) for i in range(size)])]
    all_to_all x1, starting transfers between devices: 8.86 us -> 10.7 us  [on_device(): back = lax.all_to_all(list_grads, ('x', 'z', 'core'), 0, 0, tiled=True)]
  transfers between devices with their start and end apart: 26 -> 26, of which waited for: 12 -> 17; matrix products, arithmetic and copies ran while one was open for 7% -> 6% of each run, Pallas kernels for 5% -> 5%
where the time goes in v1:
time: 162 us; the launch traced here: 159 us
  starting transfers between devices  63.3 us (39%)
  waiting for transfers between devices  41.7 us (26%)
  local copies, waits for them, and re-layouts  23.1 us (14%)
  Pallas kernels  22.8 us (14%)
  other arithmetic  6.18 us (4%)
  between operations  2.03 us (1%)
    ppermute x11, starting transfers between devices, ring(): lax.ppermute(value, axis, [(i, (i + shift) % size) for i in range(size)])  21.7 us
    ppermute x11, waiting for transfers between devices, ring(): lax.ppermute(value, axis, [(i, (i + shift) % size) for i in range(size)])  19.3 us
    unnamed x115, local copies, waits for them, and re-layouts  18.5 us
    ppermute x11, starting transfers between devices, flip(): return lax.ppermute(value, axis, [(i, i ^ bit) for i in range(size)])  13.8 us
    all_to_all x1, starting transfers between devices, on_device(): back = lax.all_to_all(list_grads, ('x', 'z', 'core'), 0, 0, tiled=True)  10.7 us
    all_to_all x1, starting transfers between devices, on_device(): got = lax.all_to_all(sent, ('x', 'z', 'core'), 0, 0, tiled=True)  9.25 us
    pallas_call x1, Pallas kernels, on_device(): call(forward_body, (sds((width, samples)), sds((1, samples)), sds(full, b...  9.11 us
    all_to_all x1, waiting for transfers between devices, on_device(): back = lax.all_to_all(list_grads, ('x', 'z', 'core'), 0, 0, tiled=True)  8.24 us
  transfers between devices with their start and end apart: 26, of which 17 were waited for; matrix products, arithmetic and copies ran while one was open for 6% of the time, Pallas kernels for 5%

profile of v1, /device:TPU:2, one launch (start us, length us, event | category | flops | bytes accessed | tf_op | source)
XLA Modules:
  0.0 159.0 jit_solution(8783817048500171588)
XLA Ops:
  2.5 1.2 collective-permute-done.1
  3.7 2.0 %collective-permute-start.2 = (bf16[24,1536]{1,0:T(8,128)(2,1)S(1)}, bf16[24,1536]{1,0:T(8,128)(2,1)S(1)}, u32[]{:S(2)}, u32[]{:S(2)}) collective-permute-start(bf16[24,1536]{1,0:T(8,128)(2,1)S(1)} %pad_maximum_fusion.2), channel_id=1, source_target_pairs={{0,2},{2,4},{4,6},{6,8},{8,10},{10,12},{12,14},{14,0},{1,3},{3,5},... | collective-permute-start | bytes 221192 | tf_op jit(solution)/shard_map/ppermute | solution.py:279
  5.7 4.0 %collective-permute-start.3 = (bf16[24,1536]{1,0:T(8,128)(2,1)S(1)}, bf16[24,1536]{1,0:T(8,128)(2,1)S(1)}, u32[]{:S(2)}, u32[]{:S(2)}) collective-permute-start(bf16[24,1536]{1,0:T(8,128)(2,1)S(1)} %pad_maximum_fusion.2), channel_id=1, source_target_pairs={{0,14},{2,0},{4,2},{6,4},{8,6},{10,8},{12,10},{14,12},{1,15},{3,1}... | collective-permute-start | bytes 221192 | tf_op jit(solution)/shard_map/ppermute | solution.py:279
  9.7 2.5 %collective-permute-done.2 = bf16[24,1536]{1,0:T(8,128)(2,1)S(1)} collective-permute-done((bf16[24,1536]{1,0:T(8,128)(2,1)S(1)}, bf16[24,1536]{1,0:T(8,128)(2,1)S(1)}, u32[]{:S(2)}, u32[]{:S(2)}) %collective-permute-start.2) | collective-permute-done | bytes 73760 | tf_op jit(solution)/shard_map/ppermute | solution.py:279
  12.3 4.9 %collective-permute-start.4 = (bf16[72,1536]{1,0:T(8,128)(2,1)S(1)}, bf16[72,1536]{1,0:T(8,128)(2,1)S(1)}, u32[]{:S(2)}, u32[]{:S(2)}) collective-permute-start(bf16[72,1536]{1,0:T(8,128)(2,1)S(1)} %pad_maximum_fusion), channel_id=1, source_target_pairs={{0,6},{2,8},{4,10},{6,12},{8,14},{10,0},{12,2},{14,4},{1,7},{3,9},... | collective-permute-start | bytes 663560 | tf_op jit(solution)/shard_map/ppermute | solution.py:279
  18.3 1.5 shard_map.246
  20.7 9.2 %all-to-all-start = ((f16[64,4,384]{2,1,0:T(4,128)(2,1)}), f16[64,4,384]{2,1,0:T(4,128)(2,1)S(1)}, u32[]{:S(2)}, u32[]{:S(2)}) async-start(f16[64,4,384]{2,1,0:T(4,128)(2,1)} %reshape.59), calls=%async_computation | async-start | bytes 393216 | tf_op jit(solution)/shard_map/all_to_all | solution.py:338
  31.1 1.6 collective-permute-start.6
  35.3 5.0 %all-to-all-done = f16[64,4,384]{2,1,0:T(4,128)(2,1)S(1)} async-done(((f16[64,4,384]{2,1,0:T(4,128)(2,1)}), f16[64,4,384]{2,1,0:T(4,128)(2,1)S(1)}, u32[]{:S(2)}, u32[]{:S(2)}) %all-to-all-start) | async-done | bytes 196640 | tf_op jit(solution)/shard_map/all_to_all | solution.py:338
  41.2 4.5 %all-to-all-start.1 = ((f16[8,48,256]{2,1,0:T(8,128)(2,1)}), f16[8,48,256]{2,1,0:T(8,128)(2,1)S(1)}, u32[]{:S(2)}, u32[]{:S(2)}) async-start(f16[8,48,256]{2,1,0:T(8,128)(2,1)} %bitcast.8), calls=%async_computation.1 | async-start | bytes 393216 | tf_op jit(solution)/shard_map/all_to_all | solution.py:340
  45.7 1.8 %collective-permute-done.6.xp_ref = bf16[192,1536]{1,0:T(8,128)(2,1)S(1)} collective-permute-done((bf16[192,1536]{1,0:T(8,128)(2,1)S(1)}, bf16[192,1536]{1,0:T(8,128)(2,1)S(1)}, u32[]{:S(2)}, u32[]{:S(2)}) %collective-permute-start.6) | collective-permute-done | bytes 589856 | tf_op jit(solution)/shard_map/ppermute | solution.py:279
  47.6 1.6 %collective-permute-start.8 = (bf16[96,1536]{1,0:T(8,128)(2,1)S(1)}, bf16[96,1536]{1,0:T(8,128)(2,1)S(1)}, u32[]{:S(2)}, u32[]{:S(2)}) collective-permute-start(bf16[96,1536]{1,0:T(8,128)(2,1)S(1)} %slice.76), channel_id=1, source_target_pairs={{0,16},{16,32},{32,48},{48,0},{1,17},{17,33},{33,49},{49,1},{2,18}... | collective-permute-start | bytes 884744 | tf_op jit(solution)/shard_map/ppermute | solution.py:279
  50.0 1.0 bitcast_convert_fusion.1.own_ref
  50.9 1.6 all-to-all-done.1
  52.6 3.0 %collective-permute-done.8.xa_ref = bf16[96,1536]{1,0:T(8,128)(2,1)S(1)} collective-permute-done((bf16[96,1536]{1,0:T(8,128)(2,1)S(1)}, bf16[96,1536]{1,0:T(8,128)(2,1)S(1)}, u32[]{:S(2)}, u32[]{:S(2)}) %collective-permute-start.8) | collective-permute-done | bytes 294944 | tf_op jit(solution)/shard_map/ppermute | solution.py:279
  56.3 0.9 collective-permute-done.9.xb_ref
  58.0 1.1 copy-done.7
  60.0 1.1 copy-done.12
  61.1 1.1 copy-done.14
  63.6 1.0 copy-done.25
  64.5 1.0 copy-done.27
  65.5 9.1 %shard_map.247 = (f32[384,512]{1,0:T(8,128)S(1)}, f32[1,512]{1,0:T(1,128)S(1)}, bf16[512,1536]{1,0:T(8,128)(2,1)S(1)}, f32[512,1536]{1,0:T(8,128)S(1)}, f32[384,...) custom-call(s32[1]{0:T(128)} %bitcast.4.where_ref, ...), custom_call_target="tpu_custom_call" | custom-call | flops 4000000000 | bytes 10000000 | tf_op jit(solution)/shard_map/pallas_call | solution.py:372
  74.6 1.0 copy-done
  75.7 1.0 copy-done.2
  76.7 0.9 copy-done.4
  77.6 1.1 copy-done.34
  79.7 1.1 collective-permute-done.10
  81.4 1.6 collective-permute-start.11
  83.0 2.9 %collective-permute-start.12 = (f32[1,512]{1,0:T(1,128)}, f32[1,512]{1,0:T(1,128)}, u32[]{:S(2)}, u32[]{:S(2)}) collective-permute-start(f32[1,512]{1,0:T(1,128)} %add.107), channel_id=1, source_target_pairs={{0,128},{64,192},{128,0},{192,64},{1,129},{65,193},{129,1},{193,65... | collective-permute-start | bytes 6152 | tf_op jit(solution)/shard_map/ppermute | solution.py:283
  88.4 2.6 %collective-permute-done.13 = f32[1,512]{1,0:T(1,128)} collective-permute-done((f32[1,512]{1,0:T(1,128)}, f32[1,512]{1,0:T(1,128)}, u32[]{:S(2)}, u32[]{:S(2)}) %collective-permute-start.13) | collective-permute-done | bytes 2080 | tf_op jit(solution)/shard_map/ppermute | solution.py:283
  91.7 1.4 copy-done.35
  93.1 3.0 %shard_map.249 = (f32[384,512]{1,0:T(8,128)S(1)}, bf16[512,384]{1,0:T(8,128)(2,1)S(1)}, f32[192,768]{1,0:T(8,128)S(1)}, bf16[192,768]{1,0:T(8,128)(2,1)S(1)}, bf...) custom-call(bf16[2,768,384]{2,1,0:T(8,128)(2,1)S(1)} %shard_map.248.place_ref, ...), custom_call_target="tpu_custom_call" | custom-call | flops 2000000000 | bytes 5000000 | tf_op jit(solution)/shard_map/pallas_call | solution.py:389
  96.2 1.3 collective-permute-start.14
  97.5 2.8 %collective-permute-start.15 = (bf16[192,768]{1,0:T(8,128)(2,1)S(1)}, bf16[192,768]{1,0:T(8,128)(2,1)S(1)}, u32[]{:S(2)}, u32[]{:S(2)}) collective-permute-start(bf16[192,768]{1,0:T(8,128)(2,1)S(1)} %get-tuple-element.42), channel_id=1, source_target_pairs={{0,32},{16,48},{32,0},{48,16},{1,33},{17,49},{33,1},{49,17},{2,34}... | collective-permute-start | bytes 884744 | tf_op jit(solution)/shard_map/ppermute | solution.py:279
  100.3 1.9 %collective-permute-start.16 = (bf16[192,768]{1,0:T(8,128)(2,1)S(1)}, bf16[192,768]{1,0:T(8,128)(2,1)S(1)}, u32[]{:S(2)}, u32[]{:S(2)}) collective-permute-start(bf16[192,768]{1,0:T(8,128)(2,1)S(1)} %get-tuple-element.43), channel_id=1, source_target_pairs={{0,48},{16,0},{32,16},{48,32},{1,49},{17,1},{33,17},{49,33},{2,50}... | collective-permute-start | bytes 884744 | tf_op jit(solution)/shard_map/ppermute | solution.py:279
  102.2 3.9 %collective-permute-done.14 = bf16[192,768]{1,0:T(8,128)(2,1)S(1)} collective-permute-done((bf16[192,768]{1,0:T(8,128)(2,1)S(1)}, bf16[192,768]{1,0:T(8,128)(2,1)S(1)}, u32[]{:S(2)}, u32[]{:S(2)}) %collective-permute-start.14) | collective-permute-done | bytes 294944 | tf_op jit(solution)/shard_map/ppermute | solution.py:279
  106.1 2.8 %collective-permute-done.15 = bf16[192,768]{1,0:T(8,128)(2,1)S(1)} collective-permute-done((bf16[192,768]{1,0:T(8,128)(2,1)S(1)}, bf16[192,768]{1,0:T(8,128)(2,1)S(1)}, u32[]{:S(2)}, u32[]{:S(2)}) %collective-permute-start.15) | collective-permute-done | bytes 294944 | tf_op jit(solution)/shard_map/ppermute | solution.py:279
  108.9 3.5 %collective-permute-done.16 = bf16[192,768]{1,0:T(8,128)(2,1)S(1)} collective-permute-done((bf16[192,768]{1,0:T(8,128)(2,1)S(1)}, bf16[192,768]{1,0:T(8,128)(2,1)S(1)}, u32[]{:S(2)}, u32[]{:S(2)}) %collective-permute-start.16) | collective-permute-done | bytes 294944 | tf_op jit(solution)/shard_map/ppermute | solution.py:279
  113.3 1.9 %collective-permute-start.17 = (f32[48,768]{1,0:T(8,128)}, f32[48,768]{1,0:T(8,128)}, u32[]{:S(2)}, u32[]{:S(2)}) collective-permute-start(f32[48,768]{1,0:T(8,128)} %get-tuple-element.58), channel_id=1, source_target_pairs={{0,2},{2,0},{4,6},{6,4},{8,10},{10,8},{12,14},{14,12},{1,3},{3,1},... | collective-permute-start | bytes 442376 | tf_op jit(solution)/shard_map/ppermute | solution.py:283
  115.3 2.2 %collective-permute-start.18 = (f32[48,768]{1,0:T(8,128)}, f32[48,768]{1,0:T(8,128)}, u32[]{:S(2)}, u32[]{:S(2)}) collective-permute-start(f32[48,768]{1,0:T(8,128)} %get-tuple-element.57), channel_id=1, source_target_pairs={{0,4},{2,6},{4,0},{6,2},{8,12},{10,14},{12,8},{14,10},{1,5},{3,7},... | collective-permute-start | bytes 442376 | tf_op jit(solution)/shard_map/ppermute | solution.py:283
  117.7 5.9 %shard_map.250 = (f32[256,384]{1,0:T(8,128)S(1)}, bf16[384,256]{1,0:T(8,128)(2,1)S(1)}) custom-call(s32[1]{0:T(128)} %bitcast.4.where_ref, s32[8,512]{1,0:T(8,128)S(1)} %get-tuple-element.24.target_ref, f32[384,512]{1,0:T(8,128)S(1)} %get-tuple-element.29.grad_sum_ref, bf16[512,384]{1,0:T(8,128)(2,1)S(1)} %get-tuple-element.30.grad_out_ref, ...), custom_call_target="tpu_custom_call" | custom-call | flops 2000000000 | bytes 8000000 | tf_op jit(solution)/shard_map/pallas_call | solution.py:405
  124.3 3.4 %all-to-all-start.2 = ((bf16[8,48,256]{2,1,0:T(8,128)(2,1)}), bf16[8,48,256]{2,1,0:T(8,128)(2,1)S(1)}, u32[]{:S(2)}, u32[]{:S(2)}) async-start(bf16[8,48,256]{2,1,0:T(8,128)(2,1)} %bitcast.28), calls=%async_computation.2 | async-start | bytes 393216 | tf_op jit(solution)/shard_map/all_to_all | solution.py:412
  127.7 1.7 %collective-permute-done.18 = f32[48,768]{1,0:T(8,128)} collective-permute-done((f32[48,768]{1,0:T(8,128)}, f32[48,768]{1,0:T(8,128)}, u32[]{:S(2)}, u32[]{:S(2)}) %collective-permute-start.18) | collective-permute-done | bytes 147488 | tf_op jit(solution)/shard_map/ppermute | solution.py:283
  129.4 1.2 fusion
  130.6 4.3 %collective-permute-start.20 = (f32[24,768]{1,0:T(8,128)S(1)}, f32[24,768]{1,0:T(8,128)S(1)}, u32[]{:S(2)}, u32[]{:S(2)}) collective-permute-start(f32[24,768]{1,0:T(8,128)S(1)} %slice.83), channel_id=1, source_target_pairs={{0,8},{2,10},{4,12},{6,14},{8,0},{10,2},{12,4},{14,6},{1,9},{3,11}... | collective-permute-start | bytes 221192 | tf_op jit(solution)/shard_map/ppermute | solution.py:283
  135.8 10.7 %all-to-all-start.3 = ((bf16[64,4,384]{2,1,0:T(4,128)(2,1)}), bf16[64,4,384]{2,1,0:T(4,128)(2,1)S(1)}, u32[]{:S(2)}, u32[]{:S(2)}) async-start(bf16[64,4,384]{2,1,0:T(4,128)(2,1)} %shard_map.251), calls=%async_computation.3 | async-start | bytes 393216 | tf_op jit(solution)/shard_map/all_to_all | solution.py:416
  148.6 8.2 %all-to-all-done.3.back_ref = bf16[64,4,384]{2,1,0:T(4,128)(2,1)S(1)} async-done(((bf16[64,4,384]{2,1,0:T(4,128)(2,1)}), bf16[64,4,384]{2,1,0:T(4,128)(2,1)S(1)}, u32[]{:S(2)}, u32[]{:S(2)}) %all-to-all-start.3) | async-done | bytes 196640 | tf_op jit(solution)/shard_map/all_to_all | solution.py:416
  156.8 2.2 %shard_map.252 = (f32[2,256,384]{2,1,0:T(8,128)}, f32[2,256]{1,0:T(2,128)}) custom-call(s32[1]{0:T(128)S(6)} %copy.46.step_ref, f32[2,256,384]{2,1,0:T(8,128)S(1)} %copy-done.23, f32[2,256]{1,0:T(2,128)S(1)} %copy-done.28, s32[2,256]{1,0:T(2,128)S(1)} %copy-done.30, s32[4,64]{1,0:T(4,128)S(1)} %bitcast.30, s32[2,64]{1,0:T(2,128)S(1)} %bitcast.31, ...), custom_call_target="tpu_custom_call" | custom-call | flops 1000000000 | bytes 3000000 | tf_op jit(solution)/shard_map/pallas_call | solution.py:417
  (164 shorter events, 21.7 us)
Async XLA Ops:
  0.6 16.9 %copy-start.42 = (s32[256]{0:T(256)S(1)}, s32[256]{0:T(256)}, u32[]{:S(2)}) copy-start(s32[256]{0:T(256)} %param.30) | copy-start | bytes 3076
  0.6 16.9 %copy-start.41 = (s32[8,256]{1,0:T(8,128)S(1)}, s32[8,256]{1,0:T(8,128)}, u32[]{:S(2)}) copy-start(s32[8,256]{1,0:T(8,128)} %param.29) | copy-start | bytes 24580
  0.7 17.6 %copy-start.31 = (s32[2,1,64,2]{2,3,1,0:T(2,128)S(1)}, s32[2,1,64,2]{2,3,1,0:T(2,128)}, u32[]{:S(2)}) copy-start(s32[2,1,64,2]{2,3,1,0:T(2,128)} %param.27) | copy-start | bytes 3076
  0.7 17.6 %copy-start.22 = (f32[2,256,384]{2,1,0:T(8,128)S(1)}, f32[2,256,384]{2,1,0:T(8,128)}, u32[]{:S(2)}) copy-start(f32[2,256,384]{2,1,0:T(8,128)} %table_ref.1) | copy-start | bytes 2359300
  0.7 17.6 %copy-start.29 = (s32[2,256]{1,0:T(2,128)S(1)}, s32[2,256]{1,0:T(2,128)}, u32[]{:S(2)}) copy-start(s32[2,256]{1,0:T(2,128)} %last_ref.1) | copy-start | bytes 6148
  2.4 1.3 collective-permute-start.1
  3.7 8.5 %collective-permute-start.2 = (bf16[24,1536]{1,0:T(8,128)(2,1)S(1)}, bf16[24,1536]{1,0:T(8,128)(2,1)S(1)}, u32[]{:S(2)}, u32[]{:S(2)}) collective-permute-start(bf16[24,1536]{1,0:T(8,128)(2,1)S(1)} %pad_maximum_fusion.2), channel_id=1, source_target_pairs={{0,2},{2,4},{4,6},{6,8},{8,10},{10,12},{12,14},{14,0},{1,3},{3,5},... | collective-permute-start | bytes 221192 | tf_op jit(solution)/shard_map/ppermute | solution.py:279
  5.7 6.5 %collective-permute-start.3 = (bf16[24,1536]{1,0:T(8,128)(2,1)S(1)}, bf16[24,1536]{1,0:T(8,128)(2,1)S(1)}, u32[]{:S(2)}, u32[]{:S(2)}) collective-permute-start(bf16[24,1536]{1,0:T(8,128)(2,1)S(1)} %pad_maximum_fusion.2), channel_id=1, source_target_pairs={{0,14},{2,0},{4,2},{6,4},{8,6},{10,8},{12,10},{14,12},{1,15},{3,1}... | collective-permute-start | bytes 221192 | tf_op jit(solution)/shard_map/ppermute | solution.py:279
  12.3 18.4 %collective-permute-start.4 = (bf16[72,1536]{1,0:T(8,128)(2,1)S(1)}, bf16[72,1536]{1,0:T(8,128)(2,1)S(1)}, u32[]{:S(2)}, u32[]{:S(2)}) collective-permute-start(bf16[72,1536]{1,0:T(8,128)(2,1)S(1)} %pad_maximum_fusion), channel_id=1, source_target_pairs={{0,6},{2,8},{4,10},{6,12},{8,14},{10,0},{12,2},{14,4},{1,7},{3,9},... | collective-permute-start | bytes 663560 | tf_op jit(solution)/shard_map/ppermute | solution.py:279
  17.2 12.7 %collective-permute-start.5 = (bf16[48,1536]{1,0:T(8,128)(2,1)S(1)}, bf16[48,1536]{1,0:T(8,128)(2,1)S(1)}, u32[]{:S(2)}, u32[]{:S(2)}) collective-permute-start(bf16[48,1536]{1,0:T(8,128)(2,1)S(1)} %pad_maximum_fusion.1), channel_id=1, source_target_pairs={{0,10},{2,12},{4,14},{6,0},{8,2},{10,4},{12,6},{14,8},{1,11},{3,13... | collective-permute-start | bytes 442376 | tf_op jit(solution)/shard_map/ppermute | solution.py:279
  17.5 17.2 %collective-permute-start = (s32[16,256]{1,0:T(8,128)S(1)}, s32[16,256]{1,0:T(8,128)S(1)}, u32[]{:S(2)}, u32[]{:S(2)}) collective-permute-start(s32[16,256]{1,0:T(8,128)S(1)} %pad_add_fusion), channel_id=1, source_target_pairs={{0,1},{1,0},{2,3},{3,2},{4,5},{5,4},{6,7},{7,6},{8,9},{9,8},{10,11... | collective-permute-start | bytes 49160 | tf_op jit(solution)/shard_map/ppermute | solution.py:283
  19.8 13.3 %copy-start.46 = (s32[768]{0:T(1024)S(1)}, s32[768]{0:T(1024)}, u32[]{:S(2)}) copy-start(s32[768]{0:T(1024)} %constant.86.clone) | copy-start | bytes 9220
  19.8 13.3 %copy-start.47 = (s32[768]{0:T(1024)S(1)}, s32[768]{0:T(1024)}, u32[]{:S(2)}) copy-start(s32[768]{0:T(1024)} %constant.87.clone) | copy-start | bytes 9220
  19.9 13.3 %copy-start.48 = (s32[768]{0:T(1024)S(1)}, s32[768]{0:T(1024)}, u32[]{:S(2)}) copy-start(s32[768]{0:T(1024)} %constant.88.clone) | copy-start | bytes 9220
  19.9 13.3 %copy-start.51 = (f32[2,384]{1,0:T(2,128)S(1)}, f32[2,384]{1,0:T(2,128)}, u32[]{:S(2)}) copy-start(f32[2,384]{1,0:T(2,128)} %param.33) | copy-start | bytes 9220
  20.7 19.6 %all-to-all-start = ((f16[64,4,384]{2,1,0:T(4,128)(2,1)}), f16[64,4,384]{2,1,0:T(4,128)(2,1)S(1)}, u32[]{:S(2)}, u32[]{:S(2)}) async-start(f16[64,4,384]{2,1,0:T(4,128)(2,1)} %reshape.59), calls=%async_computation | async-start | bytes 393216 | tf_op jit(solution)/shard_map/all_to_all | solution.py:338
  31.1 18.2 %copy-start.6 = (bf16[192,1536]{1,0:T(8,128)(2,1)}, bf16[192,1536]{1,0:T(8,128)(2,1)S(1)}, u32[]{:S(2)}) copy-start(bf16[192,1536]{1,0:T(8,128)(2,1)S(1)} %concatenate.37.z_ref) | copy-start | bytes 1769476
  31.1 16.5 %collective-permute-start.6 = (bf16[192,1536]{1,0:T(8,128)(2,1)S(1)}, bf16[192,1536]{1,0:T(8,128)(2,1)S(1)}, u32[]{:S(2)}, u32[]{:S(2)}) collective-permute-start(bf16[192,1536]{1,0:T(8,128)(2,1)S(1)} %concatenate.37.z_ref), channel_id=1, source_target_pairs={{0,16},{16,32},{32,48},{48,0},{1,17},{17,33},{33,49},{49,1},{2,18}... | collective-permute-start | bytes 1769480 | tf_op jit(solution)/shard_map/ppermute | solution.py:279
  32.6 16.6 %collective-permute-start.7 = (bf16[192,1536]{1,0:T(8,128)(2,1)S(1)}, bf16[192,1536]{1,0:T(8,128)(2,1)S(1)}, u32[]{:S(2)}, u32[]{:S(2)}) collective-permute-start(bf16[192,1536]{1,0:T(8,128)(2,1)S(1)} %concatenate.37.z_ref), channel_id=1, source_target_pairs={{0,48},{16,0},{32,16},{48,32},{1,49},{17,1},{33,17},{49,33},{2,50}... | collective-permute-start | bytes 1769480 | tf_op jit(solution)/shard_map/ppermute | solution.py:279
  41.2 11.3 %all-to-all-start.1 = ((f16[8,48,256]{2,1,0:T(8,128)(2,1)}), f16[8,48,256]{2,1,0:T(8,128)(2,1)S(1)}, u32[]{:S(2)}, u32[]{:S(2)}) async-start(f16[8,48,256]{2,1,0:T(8,128)(2,1)} %bitcast.8), calls=%async_computation.1 | async-start | bytes 393216 | tf_op jit(solution)/shard_map/all_to_all | solution.py:340
  47.6 8.0 %collective-permute-start.8 = (bf16[96,1536]{1,0:T(8,128)(2,1)S(1)}, bf16[96,1536]{1,0:T(8,128)(2,1)S(1)}, u32[]{:S(2)}, u32[]{:S(2)}) collective-permute-start(bf16[96,1536]{1,0:T(8,128)(2,1)S(1)} %slice.76), channel_id=1, source_target_pairs={{0,16},{16,32},{32,48},{48,0},{1,17},{17,33},{33,49},{49,1},{2,18}... | collective-permute-start | bytes 884744 | tf_op jit(solution)/shard_map/ppermute | solution.py:279
  49.3 8.0 %collective-permute-start.9 = (bf16[96,1536]{1,0:T(8,128)(2,1)S(1)}, bf16[96,1536]{1,0:T(8,128)(2,1)S(1)}, u32[]{:S(2)}, u32[]{:S(2)}) collective-permute-start(bf16[96,1536]{1,0:T(8,128)(2,1)S(1)} %slice.77), channel_id=1, source_target_pairs={{0,48},{16,0},{32,16},{48,32},{1,49},{17,1},{33,17},{49,33},{2,50}... | collective-permute-start | bytes 884744 | tf_op jit(solution)/shard_map/ppermute | solution.py:279
  65.5 14.2 %copy-start.43 = (s32[768]{0:T(1024)S(1)}, s32[768]{0:T(1024)}, u32[]{:S(2)}) copy-start(s32[768]{0:T(1024)} %constant.93.clone) | copy-start | bytes 9220
  65.5 14.2 %copy-start.44 = (s32[768]{0:T(1024)S(1)}, s32[768]{0:T(1024)}, u32[]{:S(2)}) copy-start(s32[768]{0:T(1024)} %constant.94.clone) | copy-start | bytes 9220
  65.5 14.2 %copy-start.45 = (s32[768]{0:T(1024)S(1)}, s32[768]{0:T(1024)}, u32[]{:S(2)}) copy-start(s32[768]{0:T(1024)} %constant.95.clone) | copy-start | bytes 9220
  65.5 14.2 %copy-start.52 = (pred[768]{0:T(1024)(128)(4,1)S(1)}, pred[768]{0:T(1024)(128)(4,1)}, u32[]{:S(2)}) copy-start(pred[768]{0:T(1024)(128)(4,1)} %constant.96.clone) | copy-start | bytes 2308
  65.5 14.2 %copy-start.53 = (pred[768]{0:T(1024)(128)(4,1)S(1)}, pred[768]{0:T(1024)(128)(4,1)}, u32[]{:S(2)}) copy-start(pred[768]{0:T(1024)(128)(4,1)} %constant.97.clone) | copy-start | bytes 2308
  79.6 1.2 collective-permute-start.10
  81.4 6.5 %collective-permute-start.11 = (f32[1,512]{1,0:T(1,128)}, f32[1,512]{1,0:T(1,128)}, u32[]{:S(2)}, u32[]{:S(2)}) collective-permute-start(f32[1,512]{1,0:T(1,128)} %add.107), channel_id=1, source_target_pairs={{0,64},{64,0},{128,192},{192,128},{1,65},{65,1},{129,193},{193,129... | collective-permute-start | bytes 6152 | tf_op jit(solution)/shard_map/ppermute | solution.py:283
  83.0 5.4 %collective-permute-start.12 = (f32[1,512]{1,0:T(1,128)}, f32[1,512]{1,0:T(1,128)}, u32[]{:S(2)}, u32[]{:S(2)}) collective-permute-start(f32[1,512]{1,0:T(1,128)} %add.107), channel_id=1, source_target_pairs={{0,128},{64,192},{128,0},{192,64},{1,129},{65,193},{129,1},{193,65... | collective-permute-start | bytes 6152 | tf_op jit(solution)/shard_map/ppermute | solution.py:283
  85.9 5.1 %collective-permute-start.13 = (f32[1,512]{1,0:T(1,128)}, f32[1,512]{1,0:T(1,128)}, u32[]{:S(2)}, u32[]{:S(2)}) collective-permute-start(f32[1,512]{1,0:T(1,128)} %add.107), channel_id=1, source_target_pairs={{0,192},{64,128},{128,64},{192,0},{1,193},{65,129},{129,65},{193,1... | collective-permute-start | bytes 6152 | tf_op jit(solution)/shard_map/ppermute | solution.py:283
  93.1 24.6 %copy-start.5 = (f32[384,512]{1,0:T(8,128)S(1)}, f32[384,512]{1,0:T(8,128)}, u32[]{:S(2)}) copy-start(f32[384,512]{1,0:T(8,128)} %copy-done.4) | copy-start | bytes 2359300
  96.2 10.0 %collective-permute-start.14 = (bf16[192,768]{1,0:T(8,128)(2,1)S(1)}, bf16[192,768]{1,0:T(8,128)(2,1)S(1)}, u32[]{:S(2)}, u32[]{:S(2)}) collective-permute-start(bf16[192,768]{1,0:T(8,128)(2,1)S(1)} %get-tuple-element.41), channel_id=1, source_target_pairs={{0,16},{16,32},{32,48},{48,0},{1,17},{17,33},{33,49},{49,1},{2,18}... | collective-permute-start | bytes 884744 | tf_op jit(solution)/shard_map/ppermute | solution.py:279
  97.5 11.4 %collective-permute-start.15 = (bf16[192,768]{1,0:T(8,128)(2,1)S(1)}, bf16[192,768]{1,0:T(8,128)(2,1)S(1)}, u32[]{:S(2)}, u32[]{:S(2)}) collective-permute-start(bf16[192,768]{1,0:T(8,128)(2,1)S(1)} %get-tuple-element.42), channel_id=1, source_target_pairs={{0,32},{16,48},{32,0},{48,16},{1,33},{17,49},{33,1},{49,17},{2,34}... | collective-permute-start | bytes 884744 | tf_op jit(solution)/shard_map/ppermute | solution.py:279
  100.3 12.2 %collective-permute-start.16 = (bf16[192,768]{1,0:T(8,128)(2,1)S(1)}, bf16[192,768]{1,0:T(8,128)(2,1)S(1)}, u32[]{:S(2)}, u32[]{:S(2)}) collective-permute-start(bf16[192,768]{1,0:T(8,128)(2,1)S(1)} %get-tuple-element.43), channel_id=1, source_target_pairs={{0,48},{16,0},{32,16},{48,32},{1,49},{17,1},{33,17},{49,33},{2,50}... | collective-permute-start | bytes 884744 | tf_op jit(solution)/shard_map/ppermute | solution.py:279
  113.3 14.4 %collective-permute-start.17 = (f32[48,768]{1,0:T(8,128)}, f32[48,768]{1,0:T(8,128)}, u32[]{:S(2)}, u32[]{:S(2)}) collective-permute-start(f32[48,768]{1,0:T(8,128)} %get-tuple-element.58), channel_id=1, source_target_pairs={{0,2},{2,0},{4,6},{6,4},{8,10},{10,8},{12,14},{14,12},{1,3},{3,1},... | collective-permute-start | bytes 442376 | tf_op jit(solution)/shard_map/ppermute | solution.py:283
  115.3 14.2 %collective-permute-start.18 = (f32[48,768]{1,0:T(8,128)}, f32[48,768]{1,0:T(8,128)}, u32[]{:S(2)}, u32[]{:S(2)}) collective-permute-start(f32[48,768]{1,0:T(8,128)} %get-tuple-element.57), channel_id=1, source_target_pairs={{0,4},{2,6},{4,0},{6,2},{8,12},{10,14},{12,8},{14,10},{1,5},{3,7},... | collective-permute-start | bytes 442376 | tf_op jit(solution)/shard_map/ppermute | solution.py:283
  117.5 11.9 %collective-permute-start.19 = (f32[48,768]{1,0:T(8,128)}, f32[48,768]{1,0:T(8,128)}, u32[]{:S(2)}, u32[]{:S(2)}) collective-permute-start(f32[48,768]{1,0:T(8,128)} %get-tuple-element.56), channel_id=1, source_target_pairs={{0,6},{2,4},{4,2},{6,0},{8,14},{10,12},{12,10},{14,8},{1,7},{3,5},... | collective-permute-start | bytes 442376 | tf_op jit(solution)/shard_map/ppermute | solution.py:283
  124.3 10.6 %all-to-all-start.2 = ((bf16[8,48,256]{2,1,0:T(8,128)(2,1)}), bf16[8,48,256]{2,1,0:T(8,128)(2,1)S(1)}, u32[]{:S(2)}, u32[]{:S(2)}) async-start(bf16[8,48,256]{2,1,0:T(8,128)(2,1)} %bitcast.28), calls=%async_computation.2 | async-start | bytes 393216 | tf_op jit(solution)/shard_map/all_to_all | solution.py:412
  127.7 19.0 %copy-start.18 = (f32[1,512]{1,0:T(1,128)S(1)}, f32[1,512]{1,0:T(1,128)}, u32[]{:S(2)}) copy-start(f32[1,512]{1,0:T(1,128)} %copy-done.17) | copy-start | bytes 6148
  130.6 26.2 %copy-start.23 = (f32[2,256,384]{2,1,0:T(8,128)S(1)}, f32[2,256,384]{2,1,0:T(8,128)}, u32[]{:S(2)}) copy-start(f32[2,256,384]{2,1,0:T(8,128)} %table_ref.1) | copy-start | bytes 2359300
  130.6 26.2 %copy-start.28 = (f32[2,256]{1,0:T(2,128)S(1)}, f32[2,256]{1,0:T(2,128)}, u32[]{:S(2)}) copy-start(f32[2,256]{1,0:T(2,128)} %accum_ref.1) | copy-start | bytes 6148
  130.6 26.2 %copy-start.30 = (s32[2,256]{1,0:T(2,128)S(1)}, s32[2,256]{1,0:T(2,128)}, u32[]{:S(2)}) copy-start(s32[2,256]{1,0:T(2,128)} %last_ref.1) | copy-start | bytes 6148
  130.6 26.2 %copy-start.32 = (s32[2,1,64,2]{2,3,1,0:T(2,128)S(1)}, s32[2,1,64,2]{2,3,1,0:T(2,128)}, u32[]{:S(2)}) copy-start(s32[2,1,64,2]{2,3,1,0:T(2,128)} %param.27) | copy-start | bytes 3076
  130.6 26.2 %copy-start.33 = (s32[2,1,64]{2,1,0:T(1,128)S(1)}, s32[2,1,64]{2,1,0:T(1,128)}, u32[]{:S(2)}) copy-start(s32[2,1,64]{2,1,0:T(1,128)} %param.28) | copy-start | bytes 1540
  130.6 15.8 %collective-permute-start.20 = (f32[24,768]{1,0:T(8,128)S(1)}, f32[24,768]{1,0:T(8,128)S(1)}, u32[]{:S(2)}, u32[]{:S(2)}) collective-permute-start(f32[24,768]{1,0:T(8,128)S(1)} %slice.83), channel_id=1, source_target_pairs={{0,8},{2,10},{4,12},{6,14},{8,0},{10,2},{12,4},{14,6},{1,9},{3,11}... | collective-permute-start | bytes 221192 | tf_op jit(solution)/shard_map/ppermute | solution.py:283
  135.8 21.0 %all-to-all-start.3 = ((bf16[64,4,384]{2,1,0:T(4,128)(2,1)}), bf16[64,4,384]{2,1,0:T(4,128)(2,1)S(1)}, u32[]{:S(2)}, u32[]{:S(2)}) async-start(bf16[64,4,384]{2,1,0:T(4,128)(2,1)} %shard_map.251), calls=%async_computation.3 | async-start | bytes 393216 | tf_op jit(solution)/shard_map/all_to_all | solution.py:416
  146.5 1.3 collective-permute-start.21
  (34 other events, 143.2 us)

commit v2 on v0

--- a/solution.py
+++ b/solution.py
@@ -79,7 +79,7 @@
     for copy in copies:
         copy.start()
     toks, rows, width = table_ref.shape
-    cols = out_ref.shape[0]
+    cols = out_ref.shape[0] * out_ref.shape[1]
     copies[0].wait()
     ids, tok, _ = slot_columns(ids_ref[...].astype(f32), cols)
     ids = ids + tok.astype(f32) * rows
@@ -97,7 +97,7 @@
         total = total + lax.dot_general(
             weights[j], table_ref[j], NN, preferred_element_type=f32, precision=lax.Precision.HIGHEST
         )
-    out_ref[...] = total
+    out_ref[...] = total.reshape(out_ref.shape)
 
 
 def list_targets(slots, half):
@@ -116,23 +116,25 @@
 
 
 def forward_body(
-    where_ref, own_ref, heads_ref, slots_ref, head_ref, order_ref, z_ref, xp_ref, xm_ref, xa_ref, xb_ref,
+    where_ref, own_ref, heads_ref, mine_ref, theirs_ref, head_ref, order_ref, z_ref, xp_ref, xm_ref, xa_ref, xb_ref,
     normed_in_ref, inv_in_ref, active_ref, slope_ref, normed_out_ref, inv_out_ref, logit_ref, up_ref, down_ref,
-    target_ref, all_ref, total_ref, input_ref, choice_ref,
+    target_ref, label_ref, all_ref, total_ref, input_ref,
 ):
     start = 0
     for ref in (z_ref, xp_ref, xm_ref, xa_ref, xb_ref):
         all_ref[start : start + ref.shape[0]] = ref[...]
         start += ref.shape[0]
     width, lists = own_ref.shape
-    samples = slots_ref.shape[1]
-    toks = slots_ref.shape[0] // 2
+    mine, theirs = mine_ref[...], theirs_ref[...]
+    first = where_ref[0] % 2 == 0
+    slots = jnp.concatenate([jnp.where(first, mine, theirs), jnp.where(first, theirs, mine)], axis=1)
+    samples = slots.shape[1]
+    toks = slots.shape[0] // 2
     head = width // toks
     rows, hidden = all_ref.shape
-    for k in range(2):
-        choice_ref[k * width : (k + 1) * width] = (iota((width, rows), 0) == order_ref[k : k + 1, :]).astype(bf16)
-    targets = list_targets(slots_ref[0:toks, :], samples // 2)
+    targets = list_targets(slots[0:toks, :], samples // 2)
     target_ref[...] = targets
+    label_ref[...] = slots[toks : toks + 1, :].astype(f32)
     row = iota((lists, samples), 0)
     mixed = []
     for t in range(toks):
@@ -148,13 +150,16 @@
     inv_in_ref[...] = inverse
     input_ref[...] = jnp.transpose(normed.astype(bf16))
     total_ref[...] = normed
+    order_up = (iota((width, rows), 0) == order_ref[0:1, :]).astype(bf16)
+    order_down = (iota((width, rows), 0) == order_ref[1:2, :]).astype(bf16)
     chunk = 256
 
     @pl.loop(0, hidden // chunk)
     def _(i):
         cols = pl.ds(pl.multiple_of(i * chunk, chunk), chunk)
-        both = dot(choice_ref[...], all_ref[:, cols]).astype(bf16)
-        up, down = both[:width], both[width:]
+        block = all_ref[:, cols]
+        up = dot(order_up, block).astype(bf16)
+        down = dot(order_down, block).astype(bf16)
         up_ref[:, cols] = up
         down_ref[:, cols] = down
         pre = dot(input_ref[...], up)
@@ -272,6 +277,13 @@
         table_out_ref[j] = jnp.where(touched, updated, table)
 
 
+def finish_body(core_ref, stay_ref, come_ref, out_ref):
+    first = core_ref[0] == 0
+    stay, come = stay_ref[...], come_ref[...]
+    out_ref[:, 0, :] = jnp.where(first, stay, come)
+    out_ref[:, 1, :] = jnp.where(first, come, stay)
+
+
 def ring(value, axis, size, shift):
     return lax.ppermute(value, axis, [(i, (i + shift) % size) for i in range(size)])
 
@@ -323,7 +335,7 @@
     ids = row_ids[:, 0].transpose(0, 2, 1).reshape(2 * capacity, groups)
     looked = call(
         lookup_body,
-        sds((lists, width)),
+        sds((groups, 2 * capacity, width)),
         "lookup",
         scratch=(
             pltpu.VMEM(row_table.shape, f32), pltpu.VMEM(last_step.shape, i32), pltpu.VMEM(ids.shape, i32),
@@ -331,7 +343,7 @@
         ),
         n_in=4, smem=1, flops=10**9, nbytes=2 * 10**6, away=3, room=48,
     )(step_now, row_table, last_step, ids)
-    sent = looked.astype(f16).reshape(groups, 2 * capacity, width)
+    sent = looked.astype(f16)
     got = lax.all_to_all(sent, ("x", "z", "core"), 0, 0, tiled=True)
     own = got.reshape(lists, width).T
     heads = lax.all_to_all(own.reshape(toks, head, lists), ("tok", "core"), 0, 0, tiled=True)
@@ -345,8 +357,6 @@
 
     mine = jnp.concatenate([sample_slots, labels[None], jnp.zeros((toks - 1, batch), i32)], axis=0)
     theirs = flip(mine, "core", 2, 1)
-    slots = jnp.where(core == 0, jnp.concatenate([mine, theirs], axis=1), jnp.concatenate([theirs, mine], axis=1))
-    label_row = slots[toks : toks + 1].astype(f32)
     before, after = ring(piece, "z", n_z, 1), ring(piece, "z", n_z, -1)
     pair = jnp.concatenate([before, piece], axis=0)
     three = jnp.concatenate([before, piece, after], axis=0)
@@ -367,19 +377,19 @@
     head_weight = jnp.where(core == 0, out_weight[0], out_weight[1])[:, None]
     full = (samples, hidden)
     weight = sds((width, hidden), bf16)
-    normed_in, inv_in, active, slope, normed_out, inv_out, partial, up, down, targets = call(
+    normed_in, inv_in, active, slope, normed_out, inv_out, partial, up, down, targets, label_row = call(
         forward_body,
         (
             sds((width, samples)), sds((1, samples)), sds(full, bf16), sds(full),
             sds((width, samples)), sds((1, samples)), sds((1, samples)), weight, weight, sds((toks, samples), i32),
+            sds((1, samples)),
         ),
         "forward",
         scratch=(
             pltpu.VMEM((4 * part, hidden), bf16), pltpu.VMEM((width, samples), f32), pltpu.VMEM((samples, width), bf16),
-            pltpu.VMEM((2 * width, 4 * part), bf16),
         ),
-        n_in=11, smem=1, flops=4 * 10**9, nbytes=10**7, room=24,
-    )(where, own, heads, slots, head_weight, order, line, x_before, x_after, far_a, far_b)
+        n_in=12, smem=1, flops=4 * 10**9, nbytes=10**7, room=40,
+    )(where, own, heads, mine, theirs, head_weight, order, line, x_before, x_after, far_a, far_b)
     logits = partial + flip(partial, "core", 2, 1)
     there = [flip(logits, "tok", n_tok, k) for k in (1, 2, 3)]
     logits = (logits + there[0]) + (there[1] + there[2])
@@ -424,7 +434,9 @@
     low, high = summed[:third], summed[third:]
     stay, leave = jnp.where(core == 0, low, high), jnp.where(core == 0, high, low)
     come = flip(leave, "core", 2, 1)
-    grad_down = jnp.where(core == 0, jnp.stack([stay, come], axis=1), jnp.stack([come, stay], axis=1))
+    grad_down = call(finish_body, sds(up_weight.shape), "finish", n_in=3, smem=1, flops=10**5, nbytes=10**5)(
+        core.reshape(1).astype(i32), stay, come
+    )
     logits = jnp.where(core == 0, logits[0, :batch], logits[0, batch:])
     return (new_table, new_accum, grad_down, logits)
 

time: 176 us -> 162 us (0.920)
  waiting for transfers between devices: 48.4 us -> 41.8 us
  local copies, waits for them, and re-layouts: 27.8 us -> 23.8 us
    ppermute x11, waiting for transfers between devices: 35.8 us -> 19.5 us  [ring(): lax.ppermute(value, axis, [(i, (i + shift) % size) for i in range(size)])]
    all_to_all x1, waiting for transfers between devices: 0.01 us -> 5.21 us  [on_device(): got = lax.all_to_all(sent, ('x', 'z', 'core'), 0, 0, tiled=True)]
    ppermute x11, waiting for transfers between devices: 4.41 us -> 7.76 us  [flip(): return lax.ppermute(value, axis, [(i, i ^ bit) for i in range(size)])]
    unnamed x117 -> x122, local copies, waits for them, and re-layouts: 22.1 us -> 19.1 us
  transfers between devices with their start and end apart: 26 -> 26, of which waited for: 12 -> 17; matrix products, arithmetic and copies ran while one was open for 7% -> 5% of each run, Pallas kernels for 5% -> 6%
where the time goes in v2:
time: 162 us; the launch traced here: 160 us
  starting transfers between devices  62.4 us (39%)
  waiting for transfers between devices  41.8 us (26%)
  local copies, waits for them, and re-layouts  23.8 us (15%)
  Pallas kernels  23.5 us (15%)
  other arithmetic  6.32 us (4%)
  between operations  2.07 us (1%)
    ppermute x11, starting transfers between devices, ring(): lax.ppermute(value, axis, [(i, (i + shift) % size) for i in range(size)])  21.4 us
    ppermute x11, waiting for transfers between devices, ring(): lax.ppermute(value, axis, [(i, (i + shift) % size) for i in range(size)])  19.5 us
    unnamed x122, local copies, waits for them, and re-layouts  19.1 us
    ppermute x11, starting transfers between devices, flip(): return lax.ppermute(value, axis, [(i, i ^ bit) for i in range(size)])  13.9 us
    all_to_all x1, starting transfers between devices, on_device(): back = lax.all_to_all(list_grads, ('x', 'z', 'core'), 0, 0, tiled=True)  10.1 us
    all_to_all x1, starting transfers between devices, on_device(): got = lax.all_to_all(sent, ('x', 'z', 'core'), 0, 0, tiled=True)  9.14 us
    pallas_call x1, Pallas kernels, on_device(): call(forward_body, (sds((width, samples)), sds((1, samples)), sds(full, b...  9.05 us
    all_to_all x1, waiting for transfers between devices, on_device(): back = lax.all_to_all(list_grads, ('x', 'z', 'core'), 0, 0, tiled=True)  8.29 us
  transfers between devices with their start and end apart: 26, of which 17 were waited for; matrix products, arithmetic and copies ran while one was open for 5% of the time, Pallas kernels for 6%

profile of v2, /device:TPU:2, one launch (start us, length us, event | category | flops | bytes accessed | tf_op | source)
XLA Modules:
  0.0 159.8 jit_solution(14513052576844403388)
XLA Ops:
  2.4 1.2 collective-permute-done.1
  3.7 2.0 %collective-permute-start.2 = (bf16[24,1536]{1,0:T(8,128)(2,1)S(1)}, bf16[24,1536]{1,0:T(8,128)(2,1)S(1)}, u32[]{:S(2)}, u32[]{:S(2)}) collective-permute-start(bf16[24,1536]{1,0:T(8,128)(2,1)S(1)} %pad_maximum_fusion.2), channel_id=1, source_target_pairs={{0,2},{2,4},{4,6},{6,8},{8,10},{10,12},{12,14},{14,0},{1,3},{3,5},... | collective-permute-start | bytes 221192 | tf_op jit(solution)/shard_map/ppermute | solution.py:288
  5.7 4.0 %collective-permute-start.3 = (bf16[24,1536]{1,0:T(8,128)(2,1)S(1)}, bf16[24,1536]{1,0:T(8,128)(2,1)S(1)}, u32[]{:S(2)}, u32[]{:S(2)}) collective-permute-start(bf16[24,1536]{1,0:T(8,128)(2,1)S(1)} %pad_maximum_fusion.2), channel_id=1, source_target_pairs={{0,14},{2,0},{4,2},{6,4},{8,6},{10,8},{12,10},{14,12},{1,15},{3,1}... | collective-permute-start | bytes 221192 | tf_op jit(solution)/shard_map/ppermute | solution.py:288
  9.7 2.5 %collective-permute-done.2 = bf16[24,1536]{1,0:T(8,128)(2,1)S(1)} collective-permute-done((bf16[24,1536]{1,0:T(8,128)(2,1)S(1)}, bf16[24,1536]{1,0:T(8,128)(2,1)S(1)}, u32[]{:S(2)}, u32[]{:S(2)}) %collective-permute-start.2) | collective-permute-done | bytes 73760 | tf_op jit(solution)/shard_map/ppermute | solution.py:288
  12.2 4.9 %collective-permute-start.4 = (bf16[72,1536]{1,0:T(8,128)(2,1)S(1)}, bf16[72,1536]{1,0:T(8,128)(2,1)S(1)}, u32[]{:S(2)}, u32[]{:S(2)}) collective-permute-start(bf16[72,1536]{1,0:T(8,128)(2,1)S(1)} %pad_maximum_fusion), channel_id=1, source_target_pairs={{0,6},{2,8},{4,10},{6,12},{8,14},{10,0},{12,2},{14,4},{1,7},{3,9},... | collective-permute-start | bytes 663560 | tf_op jit(solution)/shard_map/ppermute | solution.py:288
  18.1 1.5 shard_map.246
  20.6 9.1 %all-to-all-start = ((f16[64,4,384]{2,1,0:T(4,128)(2,1)}), f16[64,4,384]{2,1,0:T(4,128)(2,1)S(1)}, u32[]{:S(2)}, u32[]{:S(2)}) async-start(f16[64,4,384]{2,1,0:T(4,128)(2,1)} %convert_element_type.20), calls=%async_computation | async-start | bytes 393216 | tf_op jit(solution)/shard_map/all_to_all | solution.py:347
  31.0 1.6 collective-permute-start.6
  34.9 5.2 %all-to-all-done = f16[64,4,384]{2,1,0:T(4,128)(2,1)S(1)} async-done(((f16[64,4,384]{2,1,0:T(4,128)(2,1)}), f16[64,4,384]{2,1,0:T(4,128)(2,1)S(1)}, u32[]{:S(2)}, u32[]{:S(2)}) %all-to-all-start) | async-done | bytes 196640 | tf_op jit(solution)/shard_map/all_to_all | solution.py:347
  41.0 4.5 %all-to-all-start.1 = ((f16[8,48,256]{2,1,0:T(8,128)(2,1)}), f16[8,48,256]{2,1,0:T(8,128)(2,1)S(1)}, u32[]{:S(2)}, u32[]{:S(2)}) async-start(f16[8,48,256]{2,1,0:T(8,128)(2,1)} %bitcast.8), calls=%async_computation.1 | async-start | bytes 393216 | tf_op jit(solution)/shard_map/all_to_all | solution.py:349
  45.5 1.9 %collective-permute-done.6.xp_ref = bf16[192,1536]{1,0:T(8,128)(2,1)S(1)} collective-permute-done((bf16[192,1536]{1,0:T(8,128)(2,1)S(1)}, bf16[192,1536]{1,0:T(8,128)(2,1)S(1)}, u32[]{:S(2)}, u32[]{:S(2)}) %collective-permute-start.6) | collective-permute-done | bytes 589856 | tf_op jit(solution)/shard_map/ppermute | solution.py:288
  47.4 1.6 %collective-permute-start.8 = (bf16[96,1536]{1,0:T(8,128)(2,1)S(1)}, bf16[96,1536]{1,0:T(8,128)(2,1)S(1)}, u32[]{:S(2)}, u32[]{:S(2)}) collective-permute-start(bf16[96,1536]{1,0:T(8,128)(2,1)S(1)} %slice.76), channel_id=1, source_target_pairs={{0,16},{16,32},{32,48},{48,0},{1,17},{17,33},{33,49},{49,1},{2,18}... | collective-permute-start | bytes 884744 | tf_op jit(solution)/shard_map/ppermute | solution.py:288
  50.3 1.0 bitcast_convert_fusion.1.own_ref
  51.3 1.0 all-to-all-done.1
  52.9 2.4 %collective-permute-done.8.xa_ref = bf16[96,1536]{1,0:T(8,128)(2,1)S(1)} collective-permute-done((bf16[96,1536]{1,0:T(8,128)(2,1)S(1)}, bf16[96,1536]{1,0:T(8,128)(2,1)S(1)}, u32[]{:S(2)}, u32[]{:S(2)}) %collective-permute-start.8) | collective-permute-done | bytes 294944 | tf_op jit(solution)/shard_map/ppermute | solution.py:288
  56.0 1.6 %collective-permute-done.9.xb_ref = bf16[96,1536]{1,0:T(8,128)(2,1)S(1)} collective-permute-done((bf16[96,1536]{1,0:T(8,128)(2,1)}, bf16[96,1536]{1,0:T(8,128)(2,1)S(1)}, u32[]{:S(2)}, u32[]{:S(2)}) %collective-permute-start.9) | collective-permute-done | bytes 294944 | tf_op jit(solution)/shard_map/ppermute | solution.py:288
  58.4 1.1 copy-done.7
  59.4 0.9 copy-done.8
  60.4 1.1 copy-done.12
  61.4 1.1 copy-done.14
  63.9 1.0 copy-done.25
  64.9 1.0 copy-done.27
  66.6 9.1 %shard_map.247 = (f32[384,512]{1,0:T(8,128)S(1)}, f32[1,512]{1,0:T(1,128)S(1)}, bf16[512,1536]{1,0:T(8,128)(2,1)S(1)}, f32[512,1536]{1,0:T(8,128)S(1)}, f32[384,...) custom-call(s32[1]{0:T(128)} %bitcast.4.where_ref, ...), custom_call_target="tpu_custom_call" | custom-call | flops 4000000000 | bytes 10000000 | tf_op jit(solution)/shard_map/pallas_call | solution.py:380
  75.6 1.0 copy-done
  76.7 1.0 copy-done.2
  78.6 1.2 copy-done.36
  80.7 1.1 collective-permute-done.10
  82.4 1.6 collective-permute-start.11
  83.9 2.9 %collective-permute-start.12 = (f32[1,512]{1,0:T(1,128)}, f32[1,512]{1,0:T(1,128)}, u32[]{:S(2)}, u32[]{:S(2)}) collective-permute-start(f32[1,512]{1,0:T(1,128)} %add.107), channel_id=1, source_target_pairs={{0,128},{64,192},{128,0},{192,64},{1,129},{65,193},{129,1},{193,65... | collective-permute-start | bytes 6152 | tf_op jit(solution)/shard_map/ppermute | solution.py:292
  89.4 2.6 %collective-permute-done.13 = f32[1,512]{1,0:T(1,128)} collective-permute-done((f32[1,512]{1,0:T(1,128)}, f32[1,512]{1,0:T(1,128)}, u32[]{:S(2)}, u32[]{:S(2)}) %collective-permute-start.13) | collective-permute-done | bytes 2080 | tf_op jit(solution)/shard_map/ppermute | solution.py:292
  92.7 1.4 copy-done.37
  94.1 3.0 %shard_map.249 = (f32[384,512]{1,0:T(8,128)S(1)}, bf16[512,384]{1,0:T(8,128)(2,1)S(1)}, f32[192,768]{1,0:T(8,128)S(1)}, bf16[192,768]{1,0:T(8,128)(2,1)S(1)}, bf...) custom-call(bf16[2,768,384]{2,1,0:T(8,128)(2,1)S(1)} %shard_map.248.place_ref, ...), custom_call_target="tpu_custom_call" | custom-call | flops 2000000000 | bytes 5000000 | tf_op jit(solution)/shard_map/pallas_call | solution.py:398
  97.1 1.4 collective-permute-start.14
  98.5 2.1 %collective-permute-start.15 = (bf16[192,768]{1,0:T(8,128)(2,1)S(1)}, bf16[192,768]{1,0:T(8,128)(2,1)S(1)}, u32[]{:S(2)}, u32[]{:S(2)}) collective-permute-start(bf16[192,768]{1,0:T(8,128)(2,1)S(1)} %get-tuple-element.44), channel_id=1, source_target_pairs={{0,32},{16,48},{32,0},{48,16},{1,33},{17,49},{33,1},{49,17},{2,34}... | collective-permute-start | bytes 884744 | tf_op jit(solution)/shard_map/ppermute | solution.py:288
  100.6 2.5 %collective-permute-start.16 = (bf16[192,768]{1,0:T(8,128)(2,1)S(1)}, bf16[192,768]{1,0:T(8,128)(2,1)S(1)}, u32[]{:S(2)}, u32[]{:S(2)}) collective-permute-start(bf16[192,768]{1,0:T(8,128)(2,1)S(1)} %get-tuple-element.45), channel_id=1, source_target_pairs={{0,48},{16,0},{32,16},{48,32},{1,49},{17,1},{33,17},{49,33},{2,50}... | collective-permute-start | bytes 884744 | tf_op jit(solution)/shard_map/ppermute | solution.py:288
  103.2 3.9 %collective-permute-done.14 = bf16[192,768]{1,0:T(8,128)(2,1)S(1)} collective-permute-done((bf16[192,768]{1,0:T(8,128)(2,1)S(1)}, bf16[192,768]{1,0:T(8,128)(2,1)S(1)}, u32[]{:S(2)}, u32[]{:S(2)}) %collective-permute-start.14) | collective-permute-done | bytes 294944 | tf_op jit(solution)/shard_map/ppermute | solution.py:288
  107.1 2.8 %collective-permute-done.15 = bf16[192,768]{1,0:T(8,128)(2,1)S(1)} collective-permute-done((bf16[192,768]{1,0:T(8,128)(2,1)S(1)}, bf16[192,768]{1,0:T(8,128)(2,1)S(1)}, u32[]{:S(2)}, u32[]{:S(2)}) %collective-permute-start.15) | collective-permute-done | bytes 294944 | tf_op jit(solution)/shard_map/ppermute | solution.py:288
  109.9 3.5 %collective-permute-done.16 = bf16[192,768]{1,0:T(8,128)(2,1)S(1)} collective-permute-done((bf16[192,768]{1,0:T(8,128)(2,1)S(1)}, bf16[192,768]{1,0:T(8,128)(2,1)S(1)}, u32[]{:S(2)}, u32[]{:S(2)}) %collective-permute-start.16) | collective-permute-done | bytes 294944 | tf_op jit(solution)/shard_map/ppermute | solution.py:288
  114.4 2.0 %collective-permute-start.17 = (f32[48,768]{1,0:T(8,128)}, f32[48,768]{1,0:T(8,128)}, u32[]{:S(2)}, u32[]{:S(2)}) collective-permute-start(f32[48,768]{1,0:T(8,128)} %get-tuple-element.48), channel_id=1, source_target_pairs={{0,2},{2,0},{4,6},{6,4},{8,10},{10,8},{12,14},{14,12},{1,3},{3,1},... | collective-permute-start | bytes 442376 | tf_op jit(solution)/shard_map/ppermute | solution.py:292
  116.4 2.1 %collective-permute-start.18 = (f32[48,768]{1,0:T(8,128)}, f32[48,768]{1,0:T(8,128)}, u32[]{:S(2)}, u32[]{:S(2)}) collective-permute-start(f32[48,768]{1,0:T(8,128)} %get-tuple-element.47), channel_id=1, source_target_pairs={{0,4},{2,6},{4,0},{6,2},{8,12},{10,14},{12,8},{14,10},{1,5},{3,7},... | collective-permute-start | bytes 442376 | tf_op jit(solution)/shard_map/ppermute | solution.py:292
  118.8 5.9 %shard_map.250 = (f32[256,384]{1,0:T(8,128)S(1)}, bf16[384,256]{1,0:T(8,128)(2,1)S(1)}) custom-call(s32[1]{0:T(128)} %bitcast.4.where_ref, s32[8,512]{1,0:T(8,128)S(1)} %get-tuple-element.25.target_ref, f32[384,512]{1,0:T(8,128)S(1)} %get-tuple-element.31.grad_sum_ref, bf16[512,384]{1,0:T(8,128)(2,1)S(1)} %get-tuple-element.32.grad_out_ref, ...), custom_call_target="tpu_custom_call" | custom-call | flops 2000000000 | bytes 8000000 | tf_op jit(solution)/shard_map/pallas_call | solution.py:414
  125.4 3.4 %all-to-all-start.2 = ((bf16[8,48,256]{2,1,0:T(8,128)(2,1)}), bf16[8,48,256]{2,1,0:T(8,128)(2,1)S(1)}, u32[]{:S(2)}, u32[]{:S(2)}) async-start(bf16[8,48,256]{2,1,0:T(8,128)(2,1)} %bitcast.26), calls=%async_computation.2 | async-start | bytes 393216 | tf_op jit(solution)/shard_map/all_to_all | solution.py:421
  128.8 1.9 %collective-permute-done.18 = f32[48,768]{1,0:T(8,128)} collective-permute-done((f32[48,768]{1,0:T(8,128)}, f32[48,768]{1,0:T(8,128)}, u32[]{:S(2)}, u32[]{:S(2)}) %collective-permute-start.18) | collective-permute-done | bytes 147488 | tf_op jit(solution)/shard_map/ppermute | solution.py:292
  130.7 1.2 fusion
  131.9 4.5 %collective-permute-start.20 = (f32[24,768]{1,0:T(8,128)S(1)}, f32[24,768]{1,0:T(8,128)S(1)}, u32[]{:S(2)}, u32[]{:S(2)}) collective-permute-start(f32[24,768]{1,0:T(8,128)S(1)} %slice.83), channel_id=1, source_target_pairs={{0,8},{2,10},{4,12},{6,14},{8,0},{10,2},{12,4},{14,6},{1,9},{3,11}... | collective-permute-start | bytes 221192 | tf_op jit(solution)/shard_map/ppermute | solution.py:292
  137.2 10.1 %all-to-all-start.3 = ((bf16[64,4,384]{2,1,0:T(4,128)(2,1)}), bf16[64,4,384]{2,1,0:T(4,128)(2,1)S(1)}, u32[]{:S(2)}, u32[]{:S(2)}) async-start(bf16[64,4,384]{2,1,0:T(4,128)(2,1)} %shard_map.251), calls=%async_computation.3 | async-start | bytes 393216 | tf_op jit(solution)/shard_map/all_to_all | solution.py:425
  149.3 8.3 %all-to-all-done.3.back_ref = bf16[64,4,384]{2,1,0:T(4,128)(2,1)S(1)} async-done(((bf16[64,4,384]{2,1,0:T(4,128)(2,1)}), bf16[64,4,384]{2,1,0:T(4,128)(2,1)S(1)}, u32[]{:S(2)}, u32[]{:S(2)}) %all-to-all-start.3) | async-done | bytes 196640 | tf_op jit(solution)/shard_map/all_to_all | solution.py:425
  157.6 2.2 %shard_map.252 = (f32[2,256,384]{2,1,0:T(8,128)}, f32[2,256]{1,0:T(2,128)}) custom-call(s32[1]{0:T(128)S(6)} %copy.43.step_ref, f32[2,256,384]{2,1,0:T(8,128)S(1)} %copy-done.23, f32[2,256]{1,0:T(2,128)S(1)} %copy-done.30, s32[2,256]{1,0:T(2,128)S(1)} %copy-done.32, s32[4,64]{1,0:T(4,128)S(1)} %bitcast.28, s32[2,64]{1,0:T(2,128)S(1)} %bitcast.29, ...), custom_call_target="tpu_custom_call" | custom-call | flops 1000000000 | bytes 3000000 | tf_op jit(solution)/shard_map/pallas_call | solution.py:426
  (170 shorter events, 23.1 us)
Async XLA Ops:
  0.6 17.5 %copy-start.33 = (s32[2,1,64,2]{2,3,1,0:T(2,128)S(1)}, s32[2,1,64,2]{2,3,1,0:T(2,128)}, u32[]{:S(2)}) copy-start(s32[2,1,64,2]{2,3,1,0:T(2,128)} %param.27) | copy-start | bytes 3076
  0.6 17.5 %copy-start.22 = (f32[2,256,384]{2,1,0:T(8,128)S(1)}, f32[2,256,384]{2,1,0:T(8,128)}, u32[]{:S(2)}) copy-start(f32[2,256,384]{2,1,0:T(8,128)} %table_ref.1) | copy-start | bytes 2359300
  0.7 17.5 %copy-start.31 = (s32[2,256]{1,0:T(2,128)S(1)}, s32[2,256]{1,0:T(2,128)}, u32[]{:S(2)}) copy-start(s32[2,256]{1,0:T(2,128)} %last_ref.1) | copy-start | bytes 6148
  2.3 1.3 collective-permute-start.1
  3.7 8.5 %collective-permute-start.2 = (bf16[24,1536]{1,0:T(8,128)(2,1)S(1)}, bf16[24,1536]{1,0:T(8,128)(2,1)S(1)}, u32[]{:S(2)}, u32[]{:S(2)}) collective-permute-start(bf16[24,1536]{1,0:T(8,128)(2,1)S(1)} %pad_maximum_fusion.2), channel_id=1, source_target_pairs={{0,2},{2,4},{4,6},{6,8},{8,10},{10,12},{12,14},{14,0},{1,3},{3,5},... | collective-permute-start | bytes 221192 | tf_op jit(solution)/shard_map/ppermute | solution.py:288
  5.7 6.5 %collective-permute-start.3 = (bf16[24,1536]{1,0:T(8,128)(2,1)S(1)}, bf16[24,1536]{1,0:T(8,128)(2,1)S(1)}, u32[]{:S(2)}, u32[]{:S(2)}) collective-permute-start(bf16[24,1536]{1,0:T(8,128)(2,1)S(1)} %pad_maximum_fusion.2), channel_id=1, source_target_pairs={{0,14},{2,0},{4,2},{6,4},{8,6},{10,8},{12,10},{14,12},{1,15},{3,1}... | collective-permute-start | bytes 221192 | tf_op jit(solution)/shard_map/ppermute | solution.py:288
  12.2 18.4 %collective-permute-start.4 = (bf16[72,1536]{1,0:T(8,128)(2,1)S(1)}, bf16[72,1536]{1,0:T(8,128)(2,1)S(1)}, u32[]{:S(2)}, u32[]{:S(2)}) collective-permute-start(bf16[72,1536]{1,0:T(8,128)(2,1)S(1)} %pad_maximum_fusion), channel_id=1, source_target_pairs={{0,6},{2,8},{4,10},{6,12},{8,14},{10,0},{12,2},{14,4},{1,7},{3,9},... | collective-permute-start | bytes 663560 | tf_op jit(solution)/shard_map/ppermute | solution.py:288
  17.2 12.6 %collective-permute-start.5 = (bf16[48,1536]{1,0:T(8,128)(2,1)S(1)}, bf16[48,1536]{1,0:T(8,128)(2,1)S(1)}, u32[]{:S(2)}, u32[]{:S(2)}) collective-permute-start(bf16[48,1536]{1,0:T(8,128)(2,1)S(1)} %pad_maximum_fusion.1), channel_id=1, source_target_pairs={{0,10},{2,12},{4,14},{6,0},{8,2},{10,4},{12,6},{14,8},{1,11},{3,13... | collective-permute-start | bytes 442376 | tf_op jit(solution)/shard_map/ppermute | solution.py:288
  19.7 13.6 %copy-start.49 = (s32[768]{0:T(1024)S(1)}, s32[768]{0:T(1024)}, u32[]{:S(2)}) copy-start(s32[768]{0:T(1024)} %constant.86.clone) | copy-start | bytes 9220
  19.7 13.6 %copy-start.50 = (s32[768]{0:T(1024)S(1)}, s32[768]{0:T(1024)}, u32[]{:S(2)}) copy-start(s32[768]{0:T(1024)} %constant.87.clone) | copy-start | bytes 9220
  19.7 13.6 %copy-start.51 = (s32[768]{0:T(1024)S(1)}, s32[768]{0:T(1024)}, u32[]{:S(2)}) copy-start(s32[768]{0:T(1024)} %constant.88.clone) | copy-start | bytes 9220
  19.8 13.6 %copy-start.52 = (s32[768]{0:T(1024)S(1)}, s32[768]{0:T(1024)}, u32[]{:S(2)}) copy-start(s32[768]{0:T(1024)} %constant.89.clone) | copy-start | bytes 9220
  19.8 13.6 %copy-start.54 = (f32[2,384]{1,0:T(2,128)S(1)}, f32[2,384]{1,0:T(2,128)}, u32[]{:S(2)}) copy-start(f32[2,384]{1,0:T(2,128)} %param.33) | copy-start | bytes 9220
  20.6 19.5 %all-to-all-start = ((f16[64,4,384]{2,1,0:T(4,128)(2,1)}), f16[64,4,384]{2,1,0:T(4,128)(2,1)S(1)}, u32[]{:S(2)}, u32[]{:S(2)}) async-start(f16[64,4,384]{2,1,0:T(4,128)(2,1)} %convert_element_type.20), calls=%async_computation | async-start | bytes 393216 | tf_op jit(solution)/shard_map/all_to_all | solution.py:347
  31.0 18.8 %copy-start.6 = (bf16[192,1536]{1,0:T(8,128)(2,1)}, bf16[192,1536]{1,0:T(8,128)(2,1)S(1)}, u32[]{:S(2)}) copy-start(bf16[192,1536]{1,0:T(8,128)(2,1)S(1)} %concatenate.29.z_ref) | copy-start | bytes 1769476
  31.0 16.3 %collective-permute-start.6 = (bf16[192,1536]{1,0:T(8,128)(2,1)S(1)}, bf16[192,1536]{1,0:T(8,128)(2,1)S(1)}, u32[]{:S(2)}, u32[]{:S(2)}) collective-permute-start(bf16[192,1536]{1,0:T(8,128)(2,1)S(1)} %concatenate.29.z_ref), channel_id=1, source_target_pairs={{0,16},{16,32},{32,48},{48,0},{1,17},{17,33},{33,49},{49,1},{2,18}... | collective-permute-start | bytes 1769480 | tf_op jit(solution)/shard_map/ppermute | solution.py:288
  32.6 16.4 %collective-permute-start.7 = (bf16[192,1536]{1,0:T(8,128)(2,1)S(1)}, bf16[192,1536]{1,0:T(8,128)(2,1)S(1)}, u32[]{:S(2)}, u32[]{:S(2)}) collective-permute-start(bf16[192,1536]{1,0:T(8,128)(2,1)S(1)} %concatenate.29.z_ref), channel_id=1, source_target_pairs={{0,48},{16,0},{32,16},{48,32},{1,49},{17,1},{33,17},{49,33},{2,50}... | collective-permute-start | bytes 1769480 | tf_op jit(solution)/shard_map/ppermute | solution.py:288
  33.2 16.6 %copy-start.15 = (s32[16,256]{1,0:T(8,128)}, s32[16,256]{1,0:T(8,128)S(1)}, u32[]{:S(2)}) copy-start(s32[16,256]{1,0:T(8,128)S(1)} %add_add_fusion.1.mine_ref) | copy-start | bytes 49156
  33.2 19.1 %collective-permute-start = (s32[16,256]{1,0:T(8,128)S(1)}, s32[16,256]{1,0:T(8,128)S(1)}, u32[]{:S(2)}, u32[]{:S(2)}) collective-permute-start(s32[16,256]{1,0:T(8,128)S(1)} %add_add_fusion.1.mine_ref), channel_id=1, source_target_pairs={{0,1},{1,0},{2,3},{3,2},{4,5},{5,4},{6,7},{7,6},{8,9},{9,8},{10,11... | collective-permute-start | bytes 49160 | tf_op jit(solution)/shard_map/ppermute | solution.py:292
  41.0 11.3 %all-to-all-start.1 = ((f16[8,48,256]{2,1,0:T(8,128)(2,1)}), f16[8,48,256]{2,1,0:T(8,128)(2,1)S(1)}, u32[]{:S(2)}, u32[]{:S(2)}) async-start(f16[8,48,256]{2,1,0:T(8,128)(2,1)} %bitcast.8), calls=%async_computation.1 | async-start | bytes 393216 | tf_op jit(solution)/shard_map/all_to_all | solution.py:349
  47.4 7.9 %collective-permute-start.8 = (bf16[96,1536]{1,0:T(8,128)(2,1)S(1)}, bf16[96,1536]{1,0:T(8,128)(2,1)S(1)}, u32[]{:S(2)}, u32[]{:S(2)}) collective-permute-start(bf16[96,1536]{1,0:T(8,128)(2,1)S(1)} %slice.76), channel_id=1, source_target_pairs={{0,16},{16,32},{32,48},{48,0},{1,17},{17,33},{33,49},{49,1},{2,18}... | collective-permute-start | bytes 884744 | tf_op jit(solution)/shard_map/ppermute | solution.py:288
  49.8 7.8 %collective-permute-start.9 = (bf16[96,1536]{1,0:T(8,128)(2,1)}, bf16[96,1536]{1,0:T(8,128)(2,1)S(1)}, u32[]{:S(2)}, u32[]{:S(2)}) collective-permute-start(bf16[96,1536]{1,0:T(8,128)(2,1)} %slice.77), channel_id=1, source_target_pairs={{0,48},{16,0},{32,16},{48,32},{1,49},{17,1},{33,17},{49,33},{2,50}... | collective-permute-start | bytes 884744 | tf_op jit(solution)/shard_map/ppermute | solution.py:288
  66.5 14.1 %copy-start.46 = (s32[768]{0:T(1024)S(1)}, s32[768]{0:T(1024)}, u32[]{:S(2)}) copy-start(s32[768]{0:T(1024)} %constant.93.clone) | copy-start | bytes 9220
  66.5 14.1 %copy-start.47 = (s32[768]{0:T(1024)S(1)}, s32[768]{0:T(1024)}, u32[]{:S(2)}) copy-start(s32[768]{0:T(1024)} %constant.94.clone) | copy-start | bytes 9220
  66.6 14.1 %copy-start.48 = (s32[768]{0:T(1024)S(1)}, s32[768]{0:T(1024)}, u32[]{:S(2)}) copy-start(s32[768]{0:T(1024)} %constant.95.clone) | copy-start | bytes 9220
  66.6 14.1 %copy-start.56 = (pred[768]{0:T(1024)(128)(4,1)S(1)}, pred[768]{0:T(1024)(128)(4,1)}, u32[]{:S(2)}) copy-start(pred[768]{0:T(1024)(128)(4,1)} %constant.96.clone) | copy-start | bytes 2308
  66.6 14.1 %copy-start.57 = (pred[768]{0:T(1024)(128)(4,1)S(1)}, pred[768]{0:T(1024)(128)(4,1)}, u32[]{:S(2)}) copy-start(pred[768]{0:T(1024)(128)(4,1)} %constant.97.clone) | copy-start | bytes 2308
  80.6 1.2 collective-permute-start.10
  82.4 6.5 %collective-permute-start.11 = (f32[1,512]{1,0:T(1,128)}, f32[1,512]{1,0:T(1,128)}, u32[]{:S(2)}, u32[]{:S(2)}) collective-permute-start(f32[1,512]{1,0:T(1,128)} %add.107), channel_id=1, source_target_pairs={{0,64},{64,0},{128,192},{192,128},{1,65},{65,1},{129,193},{193,129... | collective-permute-start | bytes 6152 | tf_op jit(solution)/shard_map/ppermute | solution.py:292
  83.9 5.4 %collective-permute-start.12 = (f32[1,512]{1,0:T(1,128)}, f32[1,512]{1,0:T(1,128)}, u32[]{:S(2)}, u32[]{:S(2)}) collective-permute-start(f32[1,512]{1,0:T(1,128)} %add.107), channel_id=1, source_target_pairs={{0,128},{64,192},{128,0},{192,64},{1,129},{65,193},{129,1},{193,65... | collective-permute-start | bytes 6152 | tf_op jit(solution)/shard_map/ppermute | solution.py:292
  86.8 5.1 %collective-permute-start.13 = (f32[1,512]{1,0:T(1,128)}, f32[1,512]{1,0:T(1,128)}, u32[]{:S(2)}, u32[]{:S(2)}) collective-permute-start(f32[1,512]{1,0:T(1,128)} %add.107), channel_id=1, source_target_pairs={{0,192},{64,128},{128,64},{192,0},{1,193},{65,129},{129,65},{193,1... | collective-permute-start | bytes 6152 | tf_op jit(solution)/shard_map/ppermute | solution.py:292
  94.1 24.7 %copy-start.5 = (f32[384,512]{1,0:T(8,128)S(1)}, f32[384,512]{1,0:T(8,128)}, u32[]{:S(2)}) copy-start(f32[384,512]{1,0:T(8,128)} %copy-done.4) | copy-start | bytes 2359300
  97.1 10.0 %collective-permute-start.14 = (bf16[192,768]{1,0:T(8,128)(2,1)S(1)}, bf16[192,768]{1,0:T(8,128)(2,1)S(1)}, u32[]{:S(2)}, u32[]{:S(2)}) collective-permute-start(bf16[192,768]{1,0:T(8,128)(2,1)S(1)} %get-tuple-element.43), channel_id=1, source_target_pairs={{0,16},{16,32},{32,48},{48,0},{1,17},{17,33},{33,49},{49,1},{2,18}... | collective-permute-start | bytes 884744 | tf_op jit(solution)/shard_map/ppermute | solution.py:288
  98.5 11.4 %collective-permute-start.15 = (bf16[192,768]{1,0:T(8,128)(2,1)S(1)}, bf16[192,768]{1,0:T(8,128)(2,1)S(1)}, u32[]{:S(2)}, u32[]{:S(2)}) collective-permute-start(bf16[192,768]{1,0:T(8,128)(2,1)S(1)} %get-tuple-element.44), channel_id=1, source_target_pairs={{0,32},{16,48},{32,0},{48,16},{1,33},{17,49},{33,1},{49,17},{2,34}... | collective-permute-start | bytes 884744 | tf_op jit(solution)/shard_map/ppermute | solution.py:288
  100.6 12.8 %collective-permute-start.16 = (bf16[192,768]{1,0:T(8,128)(2,1)S(1)}, bf16[192,768]{1,0:T(8,128)(2,1)S(1)}, u32[]{:S(2)}, u32[]{:S(2)}) collective-permute-start(bf16[192,768]{1,0:T(8,128)(2,1)S(1)} %get-tuple-element.45), channel_id=1, source_target_pairs={{0,48},{16,0},{32,16},{48,32},{1,49},{17,1},{33,17},{49,33},{2,50}... | collective-permute-start | bytes 884744 | tf_op jit(solution)/shard_map/ppermute | solution.py:288
  114.4 14.4 %collective-permute-start.17 = (f32[48,768]{1,0:T(8,128)}, f32[48,768]{1,0:T(8,128)}, u32[]{:S(2)}, u32[]{:S(2)}) collective-permute-start(f32[48,768]{1,0:T(8,128)} %get-tuple-element.48), channel_id=1, source_target_pairs={{0,2},{2,0},{4,6},{6,4},{8,10},{10,8},{12,14},{14,12},{1,3},{3,1},... | collective-permute-start | bytes 442376 | tf_op jit(solution)/shard_map/ppermute | solution.py:292
  116.4 14.3 %collective-permute-start.18 = (f32[48,768]{1,0:T(8,128)}, f32[48,768]{1,0:T(8,128)}, u32[]{:S(2)}, u32[]{:S(2)}) collective-permute-start(f32[48,768]{1,0:T(8,128)} %get-tuple-element.47), channel_id=1, source_target_pairs={{0,4},{2,6},{4,0},{6,2},{8,12},{10,14},{12,8},{14,10},{1,5},{3,7},... | collective-permute-start | bytes 442376 | tf_op jit(solution)/shard_map/ppermute | solution.py:292
  118.5 12.1 %collective-permute-start.19 = (f32[48,768]{1,0:T(8,128)}, f32[48,768]{1,0:T(8,128)}, u32[]{:S(2)}, u32[]{:S(2)}) collective-permute-start(f32[48,768]{1,0:T(8,128)} %get-tuple-element.46), channel_id=1, source_target_pairs={{0,6},{2,4},{4,2},{6,0},{8,14},{10,12},{12,10},{14,8},{1,7},{3,5},... | collective-permute-start | bytes 442376 | tf_op jit(solution)/shard_map/ppermute | solution.py:292
  125.4 11.0 %all-to-all-start.2 = ((bf16[8,48,256]{2,1,0:T(8,128)(2,1)}), bf16[8,48,256]{2,1,0:T(8,128)(2,1)S(1)}, u32[]{:S(2)}, u32[]{:S(2)}) async-start(bf16[8,48,256]{2,1,0:T(8,128)(2,1)} %bitcast.26), calls=%async_computation.2 | async-start | bytes 393216 | tf_op jit(solution)/shard_map/all_to_all | solution.py:421
  128.8 18.8 %copy-start.18 = (f32[1,512]{1,0:T(1,128)S(1)}, f32[1,512]{1,0:T(1,128)}, u32[]{:S(2)}) copy-start(f32[1,512]{1,0:T(1,128)} %copy-done.17) | copy-start | bytes 6148
  131.8 25.8 %copy-start.23 = (f32[2,256,384]{2,1,0:T(8,128)S(1)}, f32[2,256,384]{2,1,0:T(8,128)}, u32[]{:S(2)}) copy-start(f32[2,256,384]{2,1,0:T(8,128)} %table_ref.1) | copy-start | bytes 2359300
  131.8 25.8 %copy-start.30 = (f32[2,256]{1,0:T(2,128)S(1)}, f32[2,256]{1,0:T(2,128)}, u32[]{:S(2)}) copy-start(f32[2,256]{1,0:T(2,128)} %accum_ref.1) | copy-start | bytes 6148
  131.8 25.8 %copy-start.32 = (s32[2,256]{1,0:T(2,128)S(1)}, s32[2,256]{1,0:T(2,128)}, u32[]{:S(2)}) copy-start(s32[2,256]{1,0:T(2,128)} %last_ref.1) | copy-start | bytes 6148
  131.8 25.8 %copy-start.34 = (s32[2,1,64,2]{2,3,1,0:T(2,128)S(1)}, s32[2,1,64,2]{2,3,1,0:T(2,128)}, u32[]{:S(2)}) copy-start(s32[2,1,64,2]{2,3,1,0:T(2,128)} %param.27) | copy-start | bytes 3076
  131.9 25.8 %copy-start.35 = (s32[2,1,64]{2,1,0:T(1,128)S(1)}, s32[2,1,64]{2,1,0:T(1,128)}, u32[]{:S(2)}) copy-start(s32[2,1,64]{2,1,0:T(1,128)} %param.28) | copy-start | bytes 1540
  131.9 15.4 %collective-permute-start.20 = (f32[24,768]{1,0:T(8,128)S(1)}, f32[24,768]{1,0:T(8,128)S(1)}, u32[]{:S(2)}, u32[]{:S(2)}) collective-permute-start(f32[24,768]{1,0:T(8,128)S(1)} %slice.83), channel_id=1, source_target_pairs={{0,8},{2,10},{4,12},{6,14},{8,0},{10,2},{12,4},{14,6},{1,9},{3,11}... | collective-permute-start | bytes 221192 | tf_op jit(solution)/shard_map/ppermute | solution.py:292
  137.2 20.4 %all-to-all-start.3 = ((bf16[64,4,384]{2,1,0:T(4,128)(2,1)}), bf16[64,4,384]{2,1,0:T(4,128)(2,1)S(1)}, u32[]{:S(2)}, u32[]{:S(2)}) async-start(bf16[64,4,384]{2,1,0:T(4,128)(2,1)} %shard_map.251), calls=%async_computation.3 | async-start | bytes 393216 | tf_op jit(solution)/shard_map/all_to_all | solution.py:425
  147.3 1.3 collective-permute-start.21
  (38 other events, 165.8 us)

commit v3 on v2

--- a/solution.py
+++ b/solution.py
@@ -136,12 +136,13 @@
     target_ref[...] = targets
     label_ref[...] = slots[toks : toks + 1, :].astype(f32)
     row = iota((lists, samples), 0)
+    one_own = (row == own_target(targets, where_ref[0])).astype(bf16)
+    own = dot2(own_ref[...], one_own)
     mixed = []
     for t in range(toks):
         one = (row == targets[t : t + 1, :]).astype(bf16)
         mixed.append(dot2(heads_ref[t * head : (t + 1) * head, :], one))
-    one_own = (row == own_target(targets, where_ref[0])).astype(bf16)
-    value = dot2(own_ref[...], one_own) + jnp.concatenate(mixed, axis=0)
+    value = own + jnp.concatenate(mixed, axis=0)
     centre = jnp.mean(value, axis=0, keepdims=True)
     shifted = value - centre
     inverse = lax.rsqrt(jnp.mean(shifted * shifted, axis=0, keepdims=True) + norm_eps)
@@ -149,7 +150,7 @@
     normed_in_ref[...] = normed
     inv_in_ref[...] = inverse
     input_ref[...] = jnp.transpose(normed.astype(bf16))
-    total_ref[...] = normed
+    total_ref[...] = jnp.zeros_like(total_ref)
     order_up = (iota((width, rows), 0) == order_ref[0:1, :]).astype(bf16)
     order_down = (iota((width, rows), 0) == order_ref[1:2, :]).astype(bf16)
     chunk = 256
@@ -170,7 +171,7 @@
         slope_ref[:, cols] = cumulative + pre * density
         total_ref[...] += dot(down, active, NT)
 
-    value = total_ref[...]
+    value = normed_in_ref[...] + total_ref[...]
     centre = jnp.mean(value, axis=0, keepdims=True)
     shifted = value - centre
     inverse = lax.rsqrt(jnp.mean(shifted * shifted, axis=0, keepdims=True) + norm_eps)

time: 162 us -> 162 us (level)
  no operation moved by 1% of the time
where the time goes in v3:
time: 162 us; the launch traced here: 160 us
  starting transfers between devices  62.4 us (39%)
  waiting for transfers between devices  41.8 us (26%)
  local copies, waits for them, and re-layouts  23.8 us (15%)
  Pallas kernels  23.5 us (15%)
  other arithmetic  6.32 us (4%)
  between operations  2.07 us (1%)
    ppermute x11, starting transfers between devices, ring(): lax.ppermute(value, axis, [(i, (i + shift) % size) for i in range(size)])  21.4 us
    ppermute x11, waiting for transfers between devices, ring(): lax.ppermute(value, axis, [(i, (i + shift) % size) for i in range(size)])  19.6 us
    unnamed x122, local copies, waits for them, and re-layouts  19.1 us
    ppermute x11, starting transfers between devices, flip(): return lax.ppermute(value, axis, [(i, i ^ bit) for i in range(size)])  13.9 us
    all_to_all x1, starting transfers between devices, on_device(): back = lax.all_to_all(list_grads, ('x', 'z', 'core'), 0, 0, tiled=True)  10.1 us
    all_to_all x1, starting transfers between devices, on_device(): got = lax.all_to_all(sent, ('x', 'z', 'core'), 0, 0, tiled=True)  9.14 us
    pallas_call x1, Pallas kernels, on_device(): call(forward_body, (sds((width, samples)), sds((1, samples)), sds(full, b...  9.06 us
    all_to_all x1, waiting for transfers between devices, on_device(): back = lax.all_to_all(list_grads, ('x', 'z', 'core'), 0, 0, tiled=True)  8.29 us
  transfers between devices with their start and end apart: 26, of which 17 were waited for; matrix products, arithmetic and copies ran while one was open for 5% of the time, Pallas kernels for 6%

profile of v3, /device:TPU:2, one launch (start us, length us, event | category | flops | bytes accessed | tf_op | source)
XLA Modules:
  0.0 159.8 jit_solution(10707509012377397080)
XLA Ops:
  2.4 1.2 collective-permute-done.1
  3.7 2.0 %collective-permute-start.2 = (bf16[24,1536]{1,0:T(8,128)(2,1)S(1)}, bf16[24,1536]{1,0:T(8,128)(2,1)S(1)}, u32[]{:S(2)}, u32[]{:S(2)}) collective-permute-start(bf16[24,1536]{1,0:T(8,128)(2,1)S(1)} %pad_maximum_fusion.2), channel_id=1, source_target_pairs={{0,2},{2,4},{4,6},{6,8},{8,10},{10,12},{12,14},{14,0},{1,3},{3,5},... | collective-permute-start | bytes 221192 | tf_op jit(solution)/shard_map/ppermute | solution.py:289
  5.7 4.0 %collective-permute-start.3 = (bf16[24,1536]{1,0:T(8,128)(2,1)S(1)}, bf16[24,1536]{1,0:T(8,128)(2,1)S(1)}, u32[]{:S(2)}, u32[]{:S(2)}) collective-permute-start(bf16[24,1536]{1,0:T(8,128)(2,1)S(1)} %pad_maximum_fusion.2), channel_id=1, source_target_pairs={{0,14},{2,0},{4,2},{6,4},{8,6},{10,8},{12,10},{14,12},{1,15},{3,1}... | collective-permute-start | bytes 221192 | tf_op jit(solution)/shard_map/ppermute | solution.py:289
  9.7 2.5 %collective-permute-done.2 = bf16[24,1536]{1,0:T(8,128)(2,1)S(1)} collective-permute-done((bf16[24,1536]{1,0:T(8,128)(2,1)S(1)}, bf16[24,1536]{1,0:T(8,128)(2,1)S(1)}, u32[]{:S(2)}, u32[]{:S(2)}) %collective-permute-start.2) | collective-permute-done | bytes 73760 | tf_op jit(solution)/shard_map/ppermute | solution.py:289
  12.2 4.9 %collective-permute-start.4 = (bf16[72,1536]{1,0:T(8,128)(2,1)S(1)}, bf16[72,1536]{1,0:T(8,128)(2,1)S(1)}, u32[]{:S(2)}, u32[]{:S(2)}) collective-permute-start(bf16[72,1536]{1,0:T(8,128)(2,1)S(1)} %pad_maximum_fusion), channel_id=1, source_target_pairs={{0,6},{2,8},{4,10},{6,12},{8,14},{10,0},{12,2},{14,4},{1,7},{3,9},... | collective-permute-start | bytes 663560 | tf_op jit(solution)/shard_map/ppermute | solution.py:289
  18.1 1.5 shard_map.246
  20.6 9.1 %all-to-all-start = ((f16[64,4,384]{2,1,0:T(4,128)(2,1)}), f16[64,4,384]{2,1,0:T(4,128)(2,1)S(1)}, u32[]{:S(2)}, u32[]{:S(2)}) async-start(f16[64,4,384]{2,1,0:T(4,128)(2,1)} %convert_element_type.20), calls=%async_computation | async-start | bytes 393216 | tf_op jit(solution)/shard_map/all_to_all | solution.py:348
  31.0 1.6 collective-permute-start.6
  34.9 5.2 %all-to-all-done = f16[64,4,384]{2,1,0:T(4,128)(2,1)S(1)} async-done(((f16[64,4,384]{2,1,0:T(4,128)(2,1)}), f16[64,4,384]{2,1,0:T(4,128)(2,1)S(1)}, u32[]{:S(2)}, u32[]{:S(2)}) %all-to-all-start) | async-done | bytes 196640 | tf_op jit(solution)/shard_map/all_to_all | solution.py:348
  41.0 4.5 %all-to-all-start.1 = ((f16[8,48,256]{2,1,0:T(8,128)(2,1)}), f16[8,48,256]{2,1,0:T(8,128)(2,1)S(1)}, u32[]{:S(2)}, u32[]{:S(2)}) async-start(f16[8,48,256]{2,1,0:T(8,128)(2,1)} %bitcast.8), calls=%async_computation.1 | async-start | bytes 393216 | tf_op jit(solution)/shard_map/all_to_all | solution.py:350
  45.5 1.9 %collective-permute-done.6.xp_ref = bf16[192,1536]{1,0:T(8,128)(2,1)S(1)} collective-permute-done((bf16[192,1536]{1,0:T(8,128)(2,1)S(1)}, bf16[192,1536]{1,0:T(8,128)(2,1)S(1)}, u32[]{:S(2)}, u32[]{:S(2)}) %collective-permute-start.6) | collective-permute-done | bytes 589856 | tf_op jit(solution)/shard_map/ppermute | solution.py:289
  47.4 1.6 %collective-permute-start.8 = (bf16[96,1536]{1,0:T(8,128)(2,1)S(1)}, bf16[96,1536]{1,0:T(8,128)(2,1)S(1)}, u32[]{:S(2)}, u32[]{:S(2)}) collective-permute-start(bf16[96,1536]{1,0:T(8,128)(2,1)S(1)} %slice.76), channel_id=1, source_target_pairs={{0,16},{16,32},{32,48},{48,0},{1,17},{17,33},{33,49},{49,1},{2,18}... | collective-permute-start | bytes 884744 | tf_op jit(solution)/shard_map/ppermute | solution.py:289
  50.3 1.0 bitcast_convert_fusion.1.own_ref
  51.3 1.0 all-to-all-done.1
  52.9 2.4 %collective-permute-done.8.xa_ref = bf16[96,1536]{1,0:T(8,128)(2,1)S(1)} collective-permute-done((bf16[96,1536]{1,0:T(8,128)(2,1)S(1)}, bf16[96,1536]{1,0:T(8,128)(2,1)S(1)}, u32[]{:S(2)}, u32[]{:S(2)}) %collective-permute-start.8) | collective-permute-done | bytes 294944 | tf_op jit(solution)/shard_map/ppermute | solution.py:289
  56.0 1.6 %collective-permute-done.9.xb_ref = bf16[96,1536]{1,0:T(8,128)(2,1)S(1)} collective-permute-done((bf16[96,1536]{1,0:T(8,128)(2,1)}, bf16[96,1536]{1,0:T(8,128)(2,1)S(1)}, u32[]{:S(2)}, u32[]{:S(2)}) %collective-permute-start.9) | collective-permute-done | bytes 294944 | tf_op jit(solution)/shard_map/ppermute | solution.py:289
  58.4 1.1 copy-done.7
  59.4 0.9 copy-done.8
  60.4 1.1 copy-done.12
  61.4 1.1 copy-done.14
  63.9 1.0 copy-done.25
  64.9 1.0 copy-done.27
  66.6 9.1 %shard_map.247 = (f32[384,512]{1,0:T(8,128)S(1)}, f32[1,512]{1,0:T(1,128)S(1)}, bf16[512,1536]{1,0:T(8,128)(2,1)S(1)}, f32[512,1536]{1,0:T(8,128)S(1)}, f32[384,...) custom-call(s32[1]{0:T(128)} %bitcast.4.where_ref, ...), custom_call_target="tpu_custom_call" | custom-call | flops 4000000000 | bytes 10000000 | tf_op jit(solution)/shard_map/pallas_call | solution.py:381
  75.6 1.0 copy-done
  76.7 1.0 copy-done.2
  78.6 1.2 copy-done.36
  80.7 1.1 collective-permute-done.10
  82.4 1.6 collective-permute-start.11
  83.9 2.9 %collective-permute-start.12 = (f32[1,512]{1,0:T(1,128)}, f32[1,512]{1,0:T(1,128)}, u32[]{:S(2)}, u32[]{:S(2)}) collective-permute-start(f32[1,512]{1,0:T(1,128)} %add.107), channel_id=1, source_target_pairs={{0,128},{64,192},{128,0},{192,64},{1,129},{65,193},{129,1},{193,65... | collective-permute-start | bytes 6152 | tf_op jit(solution)/shard_map/ppermute | solution.py:293
  89.3 2.6 %collective-permute-done.13 = f32[1,512]{1,0:T(1,128)} collective-permute-done((f32[1,512]{1,0:T(1,128)}, f32[1,512]{1,0:T(1,128)}, u32[]{:S(2)}, u32[]{:S(2)}) %collective-permute-start.13) | collective-permute-done | bytes 2080 | tf_op jit(solution)/shard_map/ppermute | solution.py:293
  92.7 1.4 copy-done.37
  94.1 3.0 %shard_map.249 = (f32[384,512]{1,0:T(8,128)S(1)}, bf16[512,384]{1,0:T(8,128)(2,1)S(1)}, f32[192,768]{1,0:T(8,128)S(1)}, bf16[192,768]{1,0:T(8,128)(2,1)S(1)}, bf...) custom-call(bf16[2,768,384]{2,1,0:T(8,128)(2,1)S(1)} %shard_map.248.place_ref, ...), custom_call_target="tpu_custom_call" | custom-call | flops 2000000000 | bytes 5000000 | tf_op jit(solution)/shard_map/pallas_call | solution.py:399
  97.1 1.4 collective-permute-start.14
  98.5 2.1 %collective-permute-start.15 = (bf16[192,768]{1,0:T(8,128)(2,1)S(1)}, bf16[192,768]{1,0:T(8,128)(2,1)S(1)}, u32[]{:S(2)}, u32[]{:S(2)}) collective-permute-start(bf16[192,768]{1,0:T(8,128)(2,1)S(1)} %get-tuple-element.44), channel_id=1, source_target_pairs={{0,32},{16,48},{32,0},{48,16},{1,33},{17,49},{33,1},{49,17},{2,34}... | collective-permute-start | bytes 884744 | tf_op jit(solution)/shard_map/ppermute | solution.py:289
  100.6 2.5 %collective-permute-start.16 = (bf16[192,768]{1,0:T(8,128)(2,1)S(1)}, bf16[192,768]{1,0:T(8,128)(2,1)S(1)}, u32[]{:S(2)}, u32[]{:S(2)}) collective-permute-start(bf16[192,768]{1,0:T(8,128)(2,1)S(1)} %get-tuple-element.45), channel_id=1, source_target_pairs={{0,48},{16,0},{32,16},{48,32},{1,49},{17,1},{33,17},{49,33},{2,50}... | collective-permute-start | bytes 884744 | tf_op jit(solution)/shard_map/ppermute | solution.py:289
  103.2 4.0 %collective-permute-done.14 = bf16[192,768]{1,0:T(8,128)(2,1)S(1)} collective-permute-done((bf16[192,768]{1,0:T(8,128)(2,1)S(1)}, bf16[192,768]{1,0:T(8,128)(2,1)S(1)}, u32[]{:S(2)}, u32[]{:S(2)}) %collective-permute-start.14) | collective-permute-done | bytes 294944 | tf_op jit(solution)/shard_map/ppermute | solution.py:289
  107.1 2.8 %collective-permute-done.15 = bf16[192,768]{1,0:T(8,128)(2,1)S(1)} collective-permute-done((bf16[192,768]{1,0:T(8,128)(2,1)S(1)}, bf16[192,768]{1,0:T(8,128)(2,1)S(1)}, u32[]{:S(2)}, u32[]{:S(2)}) %collective-permute-start.15) | collective-permute-done | bytes 294944 | tf_op jit(solution)/shard_map/ppermute | solution.py:289
  109.9 3.5 %collective-permute-done.16 = bf16[192,768]{1,0:T(8,128)(2,1)S(1)} collective-permute-done((bf16[192,768]{1,0:T(8,128)(2,1)S(1)}, bf16[192,768]{1,0:T(8,128)(2,1)S(1)}, u32[]{:S(2)}, u32[]{:S(2)}) %collective-permute-start.16) | collective-permute-done | bytes 294944 | tf_op jit(solution)/shard_map/ppermute | solution.py:289
  114.4 2.0 %collective-permute-start.17 = (f32[48,768]{1,0:T(8,128)}, f32[48,768]{1,0:T(8,128)}, u32[]{:S(2)}, u32[]{:S(2)}) collective-permute-start(f32[48,768]{1,0:T(8,128)} %get-tuple-element.48), channel_id=1, source_target_pairs={{0,2},{2,0},{4,6},{6,4},{8,10},{10,8},{12,14},{14,12},{1,3},{3,1},... | collective-permute-start | bytes 442376 | tf_op jit(solution)/shard_map/ppermute | solution.py:293
  116.4 2.1 %collective-permute-start.18 = (f32[48,768]{1,0:T(8,128)}, f32[48,768]{1,0:T(8,128)}, u32[]{:S(2)}, u32[]{:S(2)}) collective-permute-start(f32[48,768]{1,0:T(8,128)} %get-tuple-element.47), channel_id=1, source_target_pairs={{0,4},{2,6},{4,0},{6,2},{8,12},{10,14},{12,8},{14,10},{1,5},{3,7},... | collective-permute-start | bytes 442376 | tf_op jit(solution)/shard_map/ppermute | solution.py:293
  118.8 5.9 %shard_map.250 = (f32[256,384]{1,0:T(8,128)S(1)}, bf16[384,256]{1,0:T(8,128)(2,1)S(1)}) custom-call(s32[1]{0:T(128)} %bitcast.4.where_ref, s32[8,512]{1,0:T(8,128)S(1)} %get-tuple-element.25.target_ref, f32[384,512]{1,0:T(8,128)S(1)} %get-tuple-element.31.grad_sum_ref, bf16[512,384]{1,0:T(8,128)(2,1)S(1)} %get-tuple-element.32.grad_out_ref, ...), custom_call_target="tpu_custom_call" | custom-call | flops 2000000000 | bytes 8000000 | tf_op jit(solution)/shard_map/pallas_call | solution.py:415
  125.4 3.4 %all-to-all-start.2 = ((bf16[8,48,256]{2,1,0:T(8,128)(2,1)}), bf16[8,48,256]{2,1,0:T(8,128)(2,1)S(1)}, u32[]{:S(2)}, u32[]{:S(2)}) async-start(bf16[8,48,256]{2,1,0:T(8,128)(2,1)} %bitcast.26), calls=%async_computation.2 | async-start | bytes 393216 | tf_op jit(solution)/shard_map/all_to_all | solution.py:422
  128.8 1.9 %collective-permute-done.18 = f32[48,768]{1,0:T(8,128)} collective-permute-done((f32[48,768]{1,0:T(8,128)}, f32[48,768]{1,0:T(8,128)}, u32[]{:S(2)}, u32[]{:S(2)}) %collective-permute-start.18) | collective-permute-done | bytes 147488 | tf_op jit(solution)/shard_map/ppermute | solution.py:293
  130.7 1.2 fusion
  131.9 4.5 %collective-permute-start.20 = (f32[24,768]{1,0:T(8,128)S(1)}, f32[24,768]{1,0:T(8,128)S(1)}, u32[]{:S(2)}, u32[]{:S(2)}) collective-permute-start(f32[24,768]{1,0:T(8,128)S(1)} %slice.83), channel_id=1, source_target_pairs={{0,8},{2,10},{4,12},{6,14},{8,0},{10,2},{12,4},{14,6},{1,9},{3,11}... | collective-permute-start | bytes 221192 | tf_op jit(solution)/shard_map/ppermute | solution.py:293
  137.2 10.1 %all-to-all-start.3 = ((bf16[64,4,384]{2,1,0:T(4,128)(2,1)}), bf16[64,4,384]{2,1,0:T(4,128)(2,1)S(1)}, u32[]{:S(2)}, u32[]{:S(2)}) async-start(bf16[64,4,384]{2,1,0:T(4,128)(2,1)} %shard_map.251), calls=%async_computation.3 | async-start | bytes 393216 | tf_op jit(solution)/shard_map/all_to_all | solution.py:426
  149.3 8.3 %all-to-all-done.3.back_ref = bf16[64,4,384]{2,1,0:T(4,128)(2,1)S(1)} async-done(((bf16[64,4,384]{2,1,0:T(4,128)(2,1)}), bf16[64,4,384]{2,1,0:T(4,128)(2,1)S(1)}, u32[]{:S(2)}, u32[]{:S(2)}) %all-to-all-start.3) | async-done | bytes 196640 | tf_op jit(solution)/shard_map/all_to_all | solution.py:426
  157.6 2.2 %shard_map.252 = (f32[2,256,384]{2,1,0:T(8,128)}, f32[2,256]{1,0:T(2,128)}) custom-call(s32[1]{0:T(128)S(6)} %copy.43.step_ref, f32[2,256,384]{2,1,0:T(8,128)S(1)} %copy-done.23, f32[2,256]{1,0:T(2,128)S(1)} %copy-done.30, s32[2,256]{1,0:T(2,128)S(1)} %copy-done.32, s32[4,64]{1,0:T(4,128)S(1)} %bitcast.28, s32[2,64]{1,0:T(2,128)S(1)} %bitcast.29, ...), custom_call_target="tpu_custom_call" | custom-call | flops 1000000000 | bytes 3000000 | tf_op jit(solution)/shard_map/pallas_call | solution.py:427
  (170 shorter events, 23.1 us)
Async XLA Ops:
  0.6 17.5 %copy-start.33 = (s32[2,1,64,2]{2,3,1,0:T(2,128)S(1)}, s32[2,1,64,2]{2,3,1,0:T(2,128)}, u32[]{:S(2)}) copy-start(s32[2,1,64,2]{2,3,1,0:T(2,128)} %param.27) | copy-start | bytes 3076
  0.6 17.5 %copy-start.22 = (f32[2,256,384]{2,1,0:T(8,128)S(1)}, f32[2,256,384]{2,1,0:T(8,128)}, u32[]{:S(2)}) copy-start(f32[2,256,384]{2,1,0:T(8,128)} %table_ref.1) | copy-start | bytes 2359300
  0.7 17.5 %copy-start.31 = (s32[2,256]{1,0:T(2,128)S(1)}, s32[2,256]{1,0:T(2,128)}, u32[]{:S(2)}) copy-start(s32[2,256]{1,0:T(2,128)} %last_ref.1) | copy-start | bytes 6148
  2.3 1.3 collective-permute-start.1
  3.7 8.5 %collective-permute-start.2 = (bf16[24,1536]{1,0:T(8,128)(2,1)S(1)}, bf16[24,1536]{1,0:T(8,128)(2,1)S(1)}, u32[]{:S(2)}, u32[]{:S(2)}) collective-permute-start(bf16[24,1536]{1,0:T(8,128)(2,1)S(1)} %pad_maximum_fusion.2), channel_id=1, source_target_pairs={{0,2},{2,4},{4,6},{6,8},{8,10},{10,12},{12,14},{14,0},{1,3},{3,5},... | collective-permute-start | bytes 221192 | tf_op jit(solution)/shard_map/ppermute | solution.py:289
  5.7 6.5 %collective-permute-start.3 = (bf16[24,1536]{1,0:T(8,128)(2,1)S(1)}, bf16[24,1536]{1,0:T(8,128)(2,1)S(1)}, u32[]{:S(2)}, u32[]{:S(2)}) collective-permute-start(bf16[24,1536]{1,0:T(8,128)(2,1)S(1)} %pad_maximum_fusion.2), channel_id=1, source_target_pairs={{0,14},{2,0},{4,2},{6,4},{8,6},{10,8},{12,10},{14,12},{1,15},{3,1}... | collective-permute-start | bytes 221192 | tf_op jit(solution)/shard_map/ppermute | solution.py:289
  12.2 18.4 %collective-permute-start.4 = (bf16[72,1536]{1,0:T(8,128)(2,1)S(1)}, bf16[72,1536]{1,0:T(8,128)(2,1)S(1)}, u32[]{:S(2)}, u32[]{:S(2)}) collective-permute-start(bf16[72,1536]{1,0:T(8,128)(2,1)S(1)} %pad_maximum_fusion), channel_id=1, source_target_pairs={{0,6},{2,8},{4,10},{6,12},{8,14},{10,0},{12,2},{14,4},{1,7},{3,9},... | collective-permute-start | bytes 663560 | tf_op jit(solution)/shard_map/ppermute | solution.py:289
  17.2 12.6 %collective-permute-start.5 = (bf16[48,1536]{1,0:T(8,128)(2,1)S(1)}, bf16[48,1536]{1,0:T(8,128)(2,1)S(1)}, u32[]{:S(2)}, u32[]{:S(2)}) collective-permute-start(bf16[48,1536]{1,0:T(8,128)(2,1)S(1)} %pad_maximum_fusion.1), channel_id=1, source_target_pairs={{0,10},{2,12},{4,14},{6,0},{8,2},{10,4},{12,6},{14,8},{1,11},{3,13... | collective-permute-start | bytes 442376 | tf_op jit(solution)/shard_map/ppermute | solution.py:289
  19.7 13.6 %copy-start.49 = (s32[768]{0:T(1024)S(1)}, s32[768]{0:T(1024)}, u32[]{:S(2)}) copy-start(s32[768]{0:T(1024)} %constant.86.clone) | copy-start | bytes 9220
  19.7 13.6 %copy-start.50 = (s32[768]{0:T(1024)S(1)}, s32[768]{0:T(1024)}, u32[]{:S(2)}) copy-start(s32[768]{0:T(1024)} %constant.87.clone) | copy-start | bytes 9220
  19.7 13.6 %copy-start.51 = (s32[768]{0:T(1024)S(1)}, s32[768]{0:T(1024)}, u32[]{:S(2)}) copy-start(s32[768]{0:T(1024)} %constant.88.clone) | copy-start | bytes 9220
  19.8 13.6 %copy-start.52 = (s32[768]{0:T(1024)S(1)}, s32[768]{0:T(1024)}, u32[]{:S(2)}) copy-start(s32[768]{0:T(1024)} %constant.89.clone) | copy-start | bytes 9220
  19.8 13.6 %copy-start.54 = (f32[2,384]{1,0:T(2,128)S(1)}, f32[2,384]{1,0:T(2,128)}, u32[]{:S(2)}) copy-start(f32[2,384]{1,0:T(2,128)} %param.33) | copy-start | bytes 9220
  20.6 19.5 %all-to-all-start = ((f16[64,4,384]{2,1,0:T(4,128)(2,1)}), f16[64,4,384]{2,1,0:T(4,128)(2,1)S(1)}, u32[]{:S(2)}, u32[]{:S(2)}) async-start(f16[64,4,384]{2,1,0:T(4,128)(2,1)} %convert_element_type.20), calls=%async_computation | async-start | bytes 393216 | tf_op jit(solution)/shard_map/all_to_all | solution.py:348
  31.0 18.8 %copy-start.6 = (bf16[192,1536]{1,0:T(8,128)(2,1)}, bf16[192,1536]{1,0:T(8,128)(2,1)S(1)}, u32[]{:S(2)}) copy-start(bf16[192,1536]{1,0:T(8,128)(2,1)S(1)} %concatenate.29.z_ref) | copy-start | bytes 1769476
  31.0 16.3 %collective-permute-start.6 = (bf16[192,1536]{1,0:T(8,128)(2,1)S(1)}, bf16[192,1536]{1,0:T(8,128)(2,1)S(1)}, u32[]{:S(2)}, u32[]{:S(2)}) collective-permute-start(bf16[192,1536]{1,0:T(8,128)(2,1)S(1)} %concatenate.29.z_ref), channel_id=1, source_target_pairs={{0,16},{16,32},{32,48},{48,0},{1,17},{17,33},{33,49},{49,1},{2,18}... | collective-permute-start | bytes 1769480 | tf_op jit(solution)/shard_map/ppermute | solution.py:289
  32.6 16.4 %collective-permute-start.7 = (bf16[192,1536]{1,0:T(8,128)(2,1)S(1)}, bf16[192,1536]{1,0:T(8,128)(2,1)S(1)}, u32[]{:S(2)}, u32[]{:S(2)}) collective-permute-start(bf16[192,1536]{1,0:T(8,128)(2,1)S(1)} %concatenate.29.z_ref), channel_id=1, source_target_pairs={{0,48},{16,0},{32,16},{48,32},{1,49},{17,1},{33,17},{49,33},{2,50}... | collective-permute-start | bytes 1769480 | tf_op jit(solution)/shard_map/ppermute | solution.py:289
  33.2 16.6 %copy-start.15 = (s32[16,256]{1,0:T(8,128)}, s32[16,256]{1,0:T(8,128)S(1)}, u32[]{:S(2)}) copy-start(s32[16,256]{1,0:T(8,128)S(1)} %add_add_fusion.1.mine_ref) | copy-start | bytes 49156
  33.2 19.1 %collective-permute-start = (s32[16,256]{1,0:T(8,128)S(1)}, s32[16,256]{1,0:T(8,128)S(1)}, u32[]{:S(2)}, u32[]{:S(2)}) collective-permute-start(s32[16,256]{1,0:T(8,128)S(1)} %add_add_fusion.1.mine_ref), channel_id=1, source_target_pairs={{0,1},{1,0},{2,3},{3,2},{4,5},{5,4},{6,7},{7,6},{8,9},{9,8},{10,11... | collective-permute-start | bytes 49160 | tf_op jit(solution)/shard_map/ppermute | solution.py:293
  41.0 11.3 %all-to-all-start.1 = ((f16[8,48,256]{2,1,0:T(8,128)(2,1)}), f16[8,48,256]{2,1,0:T(8,128)(2,1)S(1)}, u32[]{:S(2)}, u32[]{:S(2)}) async-start(f16[8,48,256]{2,1,0:T(8,128)(2,1)} %bitcast.8), calls=%async_computation.1 | async-start | bytes 393216 | tf_op jit(solution)/shard_map/all_to_all | solution.py:350
  47.4 7.9 %collective-permute-start.8 = (bf16[96,1536]{1,0:T(8,128)(2,1)S(1)}, bf16[96,1536]{1,0:T(8,128)(2,1)S(1)}, u32[]{:S(2)}, u32[]{:S(2)}) collective-permute-start(bf16[96,1536]{1,0:T(8,128)(2,1)S(1)} %slice.76), channel_id=1, source_target_pairs={{0,16},{16,32},{32,48},{48,0},{1,17},{17,33},{33,49},{49,1},{2,18}... | collective-permute-start | bytes 884744 | tf_op jit(solution)/shard_map/ppermute | solution.py:289
  49.8 7.8 %collective-permute-start.9 = (bf16[96,1536]{1,0:T(8,128)(2,1)}, bf16[96,1536]{1,0:T(8,128)(2,1)S(1)}, u32[]{:S(2)}, u32[]{:S(2)}) collective-permute-start(bf16[96,1536]{1,0:T(8,128)(2,1)} %slice.77), channel_id=1, source_target_pairs={{0,48},{16,0},{32,16},{48,32},{1,49},{17,1},{33,17},{49,33},{2,50}... | collective-permute-start | bytes 884744 | tf_op jit(solution)/shard_map/ppermute | solution.py:289
  66.5 14.1 %copy-start.46 = (s32[768]{0:T(1024)S(1)}, s32[768]{0:T(1024)}, u32[]{:S(2)}) copy-start(s32[768]{0:T(1024)} %constant.93.clone) | copy-start | bytes 9220
  66.5 14.1 %copy-start.47 = (s32[768]{0:T(1024)S(1)}, s32[768]{0:T(1024)}, u32[]{:S(2)}) copy-start(s32[768]{0:T(1024)} %constant.94.clone) | copy-start | bytes 9220
  66.6 14.1 %copy-start.48 = (s32[768]{0:T(1024)S(1)}, s32[768]{0:T(1024)}, u32[]{:S(2)}) copy-start(s32[768]{0:T(1024)} %constant.95.clone) | copy-start | bytes 9220
  66.6 14.1 %copy-start.56 = (pred[768]{0:T(1024)(128)(4,1)S(1)}, pred[768]{0:T(1024)(128)(4,1)}, u32[]{:S(2)}) copy-start(pred[768]{0:T(1024)(128)(4,1)} %constant.96.clone) | copy-start | bytes 2308
  66.6 14.1 %copy-start.57 = (pred[768]{0:T(1024)(128)(4,1)S(1)}, pred[768]{0:T(1024)(128)(4,1)}, u32[]{:S(2)}) copy-start(pred[768]{0:T(1024)(128)(4,1)} %constant.97.clone) | copy-start | bytes 2308
  80.6 1.2 collective-permute-start.10
  82.4 6.5 %collective-permute-start.11 = (f32[1,512]{1,0:T(1,128)}, f32[1,512]{1,0:T(1,128)}, u32[]{:S(2)}, u32[]{:S(2)}) collective-permute-start(f32[1,512]{1,0:T(1,128)} %add.107), channel_id=1, source_target_pairs={{0,64},{64,0},{128,192},{192,128},{1,65},{65,1},{129,193},{193,129... | collective-permute-start | bytes 6152 | tf_op jit(solution)/shard_map/ppermute | solution.py:293
  83.9 5.4 %collective-permute-start.12 = (f32[1,512]{1,0:T(1,128)}, f32[1,512]{1,0:T(1,128)}, u32[]{:S(2)}, u32[]{:S(2)}) collective-permute-start(f32[1,512]{1,0:T(1,128)} %add.107), channel_id=1, source_target_pairs={{0,128},{64,192},{128,0},{192,64},{1,129},{65,193},{129,1},{193,65... | collective-permute-start | bytes 6152 | tf_op jit(solution)/shard_map/ppermute | solution.py:293
  86.8 5.1 %collective-permute-start.13 = (f32[1,512]{1,0:T(1,128)}, f32[1,512]{1,0:T(1,128)}, u32[]{:S(2)}, u32[]{:S(2)}) collective-permute-start(f32[1,512]{1,0:T(1,128)} %add.107), channel_id=1, source_target_pairs={{0,192},{64,128},{128,64},{192,0},{1,193},{65,129},{129,65},{193,1... | collective-permute-start | bytes 6152 | tf_op jit(solution)/shard_map/ppermute | solution.py:293
  94.1 24.7 %copy-start.5 = (f32[384,512]{1,0:T(8,128)S(1)}, f32[384,512]{1,0:T(8,128)}, u32[]{:S(2)}) copy-start(f32[384,512]{1,0:T(8,128)} %copy-done.4) | copy-start | bytes 2359300
  97.1 10.0 %collective-permute-start.14 = (bf16[192,768]{1,0:T(8,128)(2,1)S(1)}, bf16[192,768]{1,0:T(8,128)(2,1)S(1)}, u32[]{:S(2)}, u32[]{:S(2)}) collective-permute-start(bf16[192,768]{1,0:T(8,128)(2,1)S(1)} %get-tuple-element.43), channel_id=1, source_target_pairs={{0,16},{16,32},{32,48},{48,0},{1,17},{17,33},{33,49},{49,1},{2,18}... | collective-permute-start | bytes 884744 | tf_op jit(solution)/shard_map/ppermute | solution.py:289
  98.5 11.4 %collective-permute-start.15 = (bf16[192,768]{1,0:T(8,128)(2,1)S(1)}, bf16[192,768]{1,0:T(8,128)(2,1)S(1)}, u32[]{:S(2)}, u32[]{:S(2)}) collective-permute-start(bf16[192,768]{1,0:T(8,128)(2,1)S(1)} %get-tuple-element.44), channel_id=1, source_target_pairs={{0,32},{16,48},{32,0},{48,16},{1,33},{17,49},{33,1},{49,17},{2,34}... | collective-permute-start | bytes 884744 | tf_op jit(solution)/shard_map/ppermute | solution.py:289
  100.6 12.8 %collective-permute-start.16 = (bf16[192,768]{1,0:T(8,128)(2,1)S(1)}, bf16[192,768]{1,0:T(8,128)(2,1)S(1)}, u32[]{:S(2)}, u32[]{:S(2)}) collective-permute-start(bf16[192,768]{1,0:T(8,128)(2,1)S(1)} %get-tuple-element.45), channel_id=1, source_target_pairs={{0,48},{16,0},{32,16},{48,32},{1,49},{17,1},{33,17},{49,33},{2,50}... | collective-permute-start | bytes 884744 | tf_op jit(solution)/shard_map/ppermute | solution.py:289
  114.4 14.4 %collective-permute-start.17 = (f32[48,768]{1,0:T(8,128)}, f32[48,768]{1,0:T(8,128)}, u32[]{:S(2)}, u32[]{:S(2)}) collective-permute-start(f32[48,768]{1,0:T(8,128)} %get-tuple-element.48), channel_id=1, source_target_pairs={{0,2},{2,0},{4,6},{6,4},{8,10},{10,8},{12,14},{14,12},{1,3},{3,1},... | collective-permute-start | bytes 442376 | tf_op jit(solution)/shard_map/ppermute | solution.py:293
  116.4 14.3 %collective-permute-start.18 = (f32[48,768]{1,0:T(8,128)}, f32[48,768]{1,0:T(8,128)}, u32[]{:S(2)}, u32[]{:S(2)}) collective-permute-start(f32[48,768]{1,0:T(8,128)} %get-tuple-element.47), channel_id=1, source_target_pairs={{0,4},{2,6},{4,0},{6,2},{8,12},{10,14},{12,8},{14,10},{1,5},{3,7},... | collective-permute-start | bytes 442376 | tf_op jit(solution)/shard_map/ppermute | solution.py:293
  118.5 12.1 %collective-permute-start.19 = (f32[48,768]{1,0:T(8,128)}, f32[48,768]{1,0:T(8,128)}, u32[]{:S(2)}, u32[]{:S(2)}) collective-permute-start(f32[48,768]{1,0:T(8,128)} %get-tuple-element.46), channel_id=1, source_target_pairs={{0,6},{2,4},{4,2},{6,0},{8,14},{10,12},{12,10},{14,8},{1,7},{3,5},... | collective-permute-start | bytes 442376 | tf_op jit(solution)/shard_map/ppermute | solution.py:293
  125.4 11.0 %all-to-all-start.2 = ((bf16[8,48,256]{2,1,0:T(8,128)(2,1)}), bf16[8,48,256]{2,1,0:T(8,128)(2,1)S(1)}, u32[]{:S(2)}, u32[]{:S(2)}) async-start(bf16[8,48,256]{2,1,0:T(8,128)(2,1)} %bitcast.26), calls=%async_computation.2 | async-start | bytes 393216 | tf_op jit(solution)/shard_map/all_to_all | solution.py:422
  128.8 18.8 %copy-start.18 = (f32[1,512]{1,0:T(1,128)S(1)}, f32[1,512]{1,0:T(1,128)}, u32[]{:S(2)}) copy-start(f32[1,512]{1,0:T(1,128)} %copy-done.17) | copy-start | bytes 6148
  131.8 25.8 %copy-start.23 = (f32[2,256,384]{2,1,0:T(8,128)S(1)}, f32[2,256,384]{2,1,0:T(8,128)}, u32[]{:S(2)}) copy-start(f32[2,256,384]{2,1,0:T(8,128)} %table_ref.1) | copy-start | bytes 2359300
  131.8 25.8 %copy-start.30 = (f32[2,256]{1,0:T(2,128)S(1)}, f32[2,256]{1,0:T(2,128)}, u32[]{:S(2)}) copy-start(f32[2,256]{1,0:T(2,128)} %accum_ref.1) | copy-start | bytes 6148
  131.8 25.8 %copy-start.32 = (s32[2,256]{1,0:T(2,128)S(1)}, s32[2,256]{1,0:T(2,128)}, u32[]{:S(2)}) copy-start(s32[2,256]{1,0:T(2,128)} %last_ref.1) | copy-start | bytes 6148
  131.8 25.8 %copy-start.34 = (s32[2,1,64,2]{2,3,1,0:T(2,128)S(1)}, s32[2,1,64,2]{2,3,1,0:T(2,128)}, u32[]{:S(2)}) copy-start(s32[2,1,64,2]{2,3,1,0:T(2,128)} %param.27) | copy-start | bytes 3076
  131.9 25.8 %copy-start.35 = (s32[2,1,64]{2,1,0:T(1,128)S(1)}, s32[2,1,64]{2,1,0:T(1,128)}, u32[]{:S(2)}) copy-start(s32[2,1,64]{2,1,0:T(1,128)} %param.28) | copy-start | bytes 1540
  131.9 15.4 %collective-permute-start.20 = (f32[24,768]{1,0:T(8,128)S(1)}, f32[24,768]{1,0:T(8,128)S(1)}, u32[]{:S(2)}, u32[]{:S(2)}) collective-permute-start(f32[24,768]{1,0:T(8,128)S(1)} %slice.83), channel_id=1, source_target_pairs={{0,8},{2,10},{4,12},{6,14},{8,0},{10,2},{12,4},{14,6},{1,9},{3,11}... | collective-permute-start | bytes 221192 | tf_op jit(solution)/shard_map/ppermute | solution.py:293
  137.2 20.4 %all-to-all-start.3 = ((bf16[64,4,384]{2,1,0:T(4,128)(2,1)}), bf16[64,4,384]{2,1,0:T(4,128)(2,1)S(1)}, u32[]{:S(2)}, u32[]{:S(2)}) async-start(bf16[64,4,384]{2,1,0:T(4,128)(2,1)} %shard_map.251), calls=%async_computation.3 | async-start | bytes 393216 | tf_op jit(solution)/shard_map/all_to_all | solution.py:426
  147.3 1.3 collective-permute-start.21
  (38 other events, 165.8 us)
